TPU v7x, 512 devices: a whole 4x8x8 slice. The times are simulated.
512 devices in a mesh: img: 8 (over z), neu: 64 (over x, y, core).
Axes of the slice: x: 4, y: 8, z: 8, core: 2. Of those that a mesh axis runs over, the one named last changes fastest.
Arguments:
- image_values: bfloat16 [4096, 4096], P('neu', 'img'), may hold values from 0.25 to 16
- image_mask: int32 [4096, 4096], P('neu', 'img'), may hold values 0 or 1
- weights: bfloat16 [3, 4096, 4, 8], P(None, 'neu'), may hold values from -0.25 to 0.34960938
- block_index: int32 [3, 128, 4], P(None, 'neu'), may hold values from 0 to 511, as said below
Outputs:
- activations: bfloat16 [4096, 4096], P('neu', 'img')
- row_sums: float32 [4096], P(('img', 'neu'))
Inputs may be any that keep to these rules, and one draw needn't show every extreme that they name: Split the 512 input blocks into 64 runs of consecutive blocks, and the 128 output blocks likewise; if output block b lies in run s, block_index[l, b, k] lies in run (s + k * 16 + l) mod 64.
All inputs are finite; a program needn't handle non-finite values. No bound on the sum of `image_mask` on one device may be relied on, other than what follows from the above.
Results may differ from a plain program's by a relative error of at most 0.0035.
Values may be sent and summed in bfloat16 or wider, within the bound.
No kernel may reach another device: no remote copies, remote signals or barrier semaphores. Data moves between devices by JAX's collectives and lax.ppermute only.
A program may use at most 64 MiB of HBM per device.

v0:
```python
import jax
import jax.numpy as jnp
from jax import lax
from jax.sharding import PartitionSpec as P

KB = 4
IB = 8
OB = 32


bias_value = 0.35
ceiling = 32.0


def from_behind(block, axis, distance):
    devices = range(lax.axis_size(axis))
    route = [((i - distance) % len(devices), i) for i in devices]
    return lax.ppermute(block, axis, route)


def in_blocks(array, dim, devices):
    before, after = (array.shape[:dim], array.shape[dim + 1 :])
    return jnp.moveaxis(array.reshape(*before, devices, -1, *after), dim, 0)


def sent_and_summed(array, axis, dim):
    devices = lax.axis_size(axis)
    tiles = lax.all_to_all(in_blocks(array, dim, devices), axis, 0, 0, tiled=True)
    return jnp.sum(tiles, axis=0)


def contract(layer_weights, picked, blocks_count):
    weights_view = layer_weights.reshape(blocks_count, OB, KB * IB)
    picked_view = picked.reshape(blocks_count, KB * IB, -1)
    summed = jnp.einsum(
        "dom,dmr->dor", weights_view, picked_view, preferred_element_type=jnp.float32
    )
    clamped = jnp.minimum(jnp.maximum(summed - bias_value, 0.0), ceiling)
    return clamped.astype(jnp.bfloat16).reshape(blocks_count * OB, -1)


def on_device(image_values, image_mask, weights, block_index):
    activity = image_values * image_mask.astype(jnp.bfloat16)
    layer_count = weights.shape[0]
    blocks_count = block_index.shape[1]
    columns = activity.shape[1]
    shard_rows = activity.shape[0]
    run_blocks = shard_rows // IB
    devices = lax.axis_size("neu")
    offsets = jnp.arange(IB, dtype=jnp.int32)
    for layer_number in range(layer_count):
        layer_blocks = block_index[layer_number]
        slot_parts = []
        for slot in range(KB):
            distance = (slot * (devices // KB) + layer_number) % devices
            arrived = from_behind(activity, "neu", (devices - distance) % devices)
            local_rows = (
                (layer_blocks[:, slot] % run_blocks)[:, None] * IB + offsets[None, :]
            ).reshape(-1)
            slot_parts.append(
                jnp.take(arrived, local_rows, axis=0).reshape(blocks_count, IB, columns)
            )
        picked = jnp.stack(slot_parts, axis=1).reshape(blocks_count * KB * IB, columns)
        activity = contract(weights[layer_number], picked, blocks_count)
    partial_sums = jnp.sum(activity, axis=0, dtype=jnp.float32)
    totals = sent_and_summed(partial_sums, "neu", 0)
    return (activity, totals)


def solution(mesh):
    in_specs = (P("neu", "img"), P("neu", "img"), P(None, "neu", None, None), P(None, "neu", None))
    out_specs = (P("neu", "img"), P(("img", "neu")))
    return jax.shard_map(
        on_device, mesh=mesh, in_specs=in_specs, out_specs=out_specs, check_vma=False
    )
```

profile of v0, /device:TPU:1, one launch (start us, length us, event | category | flops | bytes accessed | tf_op | source)
XLA Modules:
  0.0 76.3 jit_solution(4272221378137676581)
XLA Ops:
  0.6 1.0 %convert_multiply_fusion = bf16[64,512]{1,0:T(8,128)(2,1)S(1)} fusion(bf16[64,512]{1,0:T(8,128)(2,1)} %param.6, s32[64,512]{1,0:T(8,128)} %param.7), kind=kLoop, calls=%fused_computation.43 | loop fusion | flops 65536 | bytes 262144 | tf_op jit(solution)/shard_map/mul | solution.py:43
  1.6 5.2 %collective-permute-start.1 = (bf16[64,512]{1,0:T(8,128)(2,1)S(1)}, bf16[64,512]{1,0:T(8,128)(2,1)S(1)}, u32[]{:S(2)}, u32[]{:S(2)}) collective-permute-start(bf16[64,512]{1,0:T(8,128)(2,1)S(1)} %convert_multiply_fusion), channel_id=1, source_target_pairs={{16,0},{17,1},{18,2},{19,3},{20,4},{21,5},{22,6},{23,7},{24,8},{25... | collective-permute-start | bytes 196616 | tf_op jit(solution)/shard_map/ppermute | solution.py:18
  6.8 2.4 %collective-permute-start.2 = (bf16[64,512]{1,0:T(8,128)(2,1)S(1)}, bf16[64,512]{1,0:T(8,128)(2,1)S(1)}, u32[]{:S(2)}, u32[]{:S(2)}) collective-permute-start(bf16[64,512]{1,0:T(8,128)(2,1)S(1)} %convert_multiply_fusion), channel_id=1, source_target_pairs={{32,0},{33,1},{34,2},{35,3},{36,4},{37,5},{38,6},{39,7},{40,8},{41... | collective-permute-start | bytes 196616 | tf_op jit(solution)/shard_map/ppermute | solution.py:18
  9.3 2.5 %collective-permute-start.3 = (bf16[64,512]{1,0:T(8,128)(2,1)S(1)}, bf16[64,512]{1,0:T(8,128)(2,1)S(1)}, u32[]{:S(2)}, u32[]{:S(2)}) collective-permute-start(bf16[64,512]{1,0:T(8,128)(2,1)S(1)} %convert_multiply_fusion), channel_id=1, source_target_pairs={{48,0},{49,1},{50,2},{51,3},{52,4},{53,5},{54,6},{55,7},{56,8},{57... | collective-permute-start | bytes 196616 | tf_op jit(solution)/shard_map/ppermute | solution.py:18
  15.5 0.6 gather_fusion
  16.2 0.6 gather_fusion.2
  16.8 0.6 gather_fusion.3
  17.7 10.1 %collective-permute-start.6 = (bf16[64,512]{1,0:T(8,128)(2,1)S(1)}, bf16[64,512]{1,0:T(8,128)(2,1)S(1)}, u32[]{:S(2)}, u32[]{:S(2)}) collective-permute-start(bf16[64,512]{1,0:T(8,128)(2,1)S(1)} %bitcast.89), channel_id=1, source_target_pairs={{33,0},{34,1},{35,2},{36,3},{37,4},{38,5},{39,6},{40,7},{41,8},{42... | collective-permute-start | bytes 196616 | tf_op jit(solution)/shard_map/ppermute | solution.py:18
  27.8 1.9 %collective-permute-start.5 = (bf16[64,512]{1,0:T(8,128)(2,1)S(1)}, bf16[64,512]{1,0:T(8,128)(2,1)S(1)}, u32[]{:S(2)}, u32[]{:S(2)}) collective-permute-start(bf16[64,512]{1,0:T(8,128)(2,1)S(1)} %bitcast.90), channel_id=1, source_target_pairs={{17,0},{18,1},{19,2},{20,3},{21,4},{22,5},{23,6},{24,7},{25,8},{26... | collective-permute-start | bytes 196616 | tf_op jit(solution)/shard_map/ppermute | solution.py:18
  29.8 1.9 %collective-permute-start.4 = (bf16[64,512]{1,0:T(8,128)(2,1)S(1)}, bf16[64,512]{1,0:T(8,128)(2,1)S(1)}, u32[]{:S(2)}, u32[]{:S(2)}) collective-permute-start(bf16[64,512]{1,0:T(8,128)(2,1)S(1)} %bitcast.91), channel_id=1, source_target_pairs={{1,0},{2,1},{3,2},{4,3},{5,4},{6,5},{7,6},{8,7},{9,8},{10,9},{11,1... | collective-permute-start | bytes 196616 | tf_op jit(solution)/shard_map/ppermute | solution.py:18
  31.7 3.3 %collective-permute-start.7 = (bf16[64,512]{1,0:T(8,128)(2,1)S(1)}, bf16[64,512]{1,0:T(8,128)(2,1)S(1)}, u32[]{:S(2)}, u32[]{:S(2)}) collective-permute-start(bf16[64,512]{1,0:T(8,128)(2,1)S(1)} %bitcast.92), channel_id=1, source_target_pairs={{49,0},{50,1},{51,2},{52,3},{53,4},{54,5},{55,6},{56,7},{57,8},{58... | collective-permute-start | bytes 196616 | tf_op jit(solution)/shard_map/ppermute | solution.py:18
  35.7 0.6 gather_fusion.5
  36.4 0.6 gather_fusion.4
  37.0 2.4 %collective-permute-done.7 = bf16[64,512]{1,0:T(8,128)(2,1)S(1)} collective-permute-done((bf16[64,512]{1,0:T(8,128)(2,1)S(1)}, bf16[64,512]{1,0:T(8,128)(2,1)S(1)}, u32[]{:S(2)}, u32[]{:S(2)}) %collective-permute-start.7) | collective-permute-done | bytes 65568 | tf_op jit(solution)/shard_map/ppermute | solution.py:18
  40.2 1.9 %collective-permute-start.10 = (bf16[64,512]{1,0:T(8,128)(2,1)S(1)}, bf16[64,512]{1,0:T(8,128)(2,1)S(1)}, u32[]{:S(2)}, u32[]{:S(2)}) collective-permute-start(bf16[64,512]{1,0:T(8,128)(2,1)S(1)} %bitcast.93), channel_id=1, source_target_pairs={{34,0},{35,1},{36,2},{37,3},{38,4},{39,5},{40,6},{41,7},{42,8},{43... | collective-permute-start | bytes 196616 | tf_op jit(solution)/shard_map/ppermute | solution.py:18
  42.2 6.8 %collective-permute-start.9 = (bf16[64,512]{1,0:T(8,128)(2,1)S(1)}, bf16[64,512]{1,0:T(8,128)(2,1)S(1)}, u32[]{:S(2)}, u32[]{:S(2)}) collective-permute-start(bf16[64,512]{1,0:T(8,128)(2,1)S(1)} %bitcast.94), channel_id=1, source_target_pairs={{18,0},{19,1},{20,2},{21,3},{22,4},{23,5},{24,6},{25,7},{26,8},{27... | collective-permute-start | bytes 196616 | tf_op jit(solution)/shard_map/ppermute | solution.py:18
  49.0 3.0 %collective-permute-start.8 = (bf16[64,512]{1,0:T(8,128)(2,1)S(1)}, bf16[64,512]{1,0:T(8,128)(2,1)S(1)}, u32[]{:S(2)}, u32[]{:S(2)}) collective-permute-start(bf16[64,512]{1,0:T(8,128)(2,1)S(1)} %bitcast.95), channel_id=1, source_target_pairs={{2,0},{3,1},{4,2},{5,3},{6,4},{7,5},{8,6},{9,7},{10,8},{11,9},{12,... | collective-permute-start | bytes 196616 | tf_op jit(solution)/shard_map/ppermute | solution.py:18
  52.0 1.9 %collective-permute-start.11 = (bf16[64,512]{1,0:T(8,128)(2,1)S(1)}, bf16[64,512]{1,0:T(8,128)(2,1)S(1)}, u32[]{:S(2)}, u32[]{:S(2)}) collective-permute-start(bf16[64,512]{1,0:T(8,128)(2,1)S(1)} %bitcast.96), channel_id=1, source_target_pairs={{50,0},{51,1},{52,2},{53,3},{54,4},{55,5},{56,6},{57,7},{58,8},{59... | collective-permute-start | bytes 196616 | tf_op jit(solution)/shard_map/ppermute | solution.py:18
  54.6 0.6 gather_fusion.9
  55.3 0.6 gather_fusion.8
  56.0 3.8 %collective-permute-done.11 = bf16[64,512]{1,0:T(8,128)(2,1)S(1)} collective-permute-done((bf16[64,512]{1,0:T(8,128)(2,1)S(1)}, bf16[64,512]{1,0:T(8,128)(2,1)S(1)}, u32[]{:S(2)}, u32[]{:S(2)}) %collective-permute-start.11) | collective-permute-done | bytes 65568 | tf_op jit(solution)/shard_map/ppermute | solution.py:18
  60.5 0.8 %convert_reduce_fusion = (f32[512]{0:T(512)S(1)}, bf16[2,512,32]{1,2,0:T(8,128)(2,1)}) fusion(bf16[2,1,8,512]{3,2,1,0:T(8,128)(2,1)S(1)} %select_bitcast_fusion, bf16[2,1,8,512]{3,2,1,0:T(8,128)(2,1)S(1)} %select_bitcast_fusion.1, bf16[2,1,8,512]{3,2,1,0:T(8,128)(2,1)S(1)} %select_bitcast_fusion.2, bf16[2,1,8,512]{3,2,1,0:T(8,128)(2,1)S(1)} %select_bitcast_fusion.3, ...), kind=kOutput, calls=%fused_computation.21 | convolution fusion | flops 2522624 | bytes 137216 | tf_op jit(solution)/shard_map/dom,dmr->dor/dot_general | solution.py:35
  61.4 14.3 %all_to_all.9 = f32[64,1,8]{2,1,0:T(1,128)S(1)} all-to-all(f32[64,1,8]{2,1,0:T(1,128)S(1)} %bitcast.88), channel_id=1, replica_groups=mesh['img'=8,'neu'=64] {'neu'}, dimensions={0} | all-to-all | bytes 4096 | tf_op jit(solution)/shard_map/all_to_all | solution.py:28
  75.7 0.6 reduce_sum.19
  (100 shorter events, 7.2 us)
Async XLA Ops:
  0.6 11.2 %copy-start.1 = (s32[3,2,4]{2,1,0:T(2,128)S(1)}, s32[3,2,4]{2,1,0:T(2,128)}, u32[]{:S(2)}) copy-start(s32[3,2,4]{2,1,0:T(2,128)} %param.9) | copy-start | bytes 292
  1.6 13.2 %collective-permute-start.1 = (bf16[64,512]{1,0:T(8,128)(2,1)S(1)}, bf16[64,512]{1,0:T(8,128)(2,1)S(1)}, u32[]{:S(2)}, u32[]{:S(2)}) collective-permute-start(bf16[64,512]{1,0:T(8,128)(2,1)S(1)} %convert_multiply_fusion), channel_id=1, source_target_pairs={{16,0},{17,1},{18,2},{19,3},{20,4},{21,5},{22,6},{23,7},{24,8},{25... | collective-permute-start | bytes 196616 | tf_op jit(solution)/shard_map/ppermute | solution.py:18
  6.8 8.7 %collective-permute-start = (bf16[64,512]{1,0:T(8,128)(2,1)S(1)}, bf16[64,512]{1,0:T(8,128)(2,1)S(1)}, u32[]{:S(2)}, u32[]{:S(2)}) collective-permute-start(bf16[64,512]{1,0:T(8,128)(2,1)S(1)} %convert_multiply_fusion), channel_id=1, source_target_pairs={{0,0},{1,1},{2,2},{3,3},{4,4},{5,5},{6,6},{7,7},{8,8},{9,9},{10,10... | collective-permute-start | bytes 196616 | tf_op jit(solution)/shard_map/ppermute | solution.py:18
  6.8 9.3 %collective-permute-start.2 = (bf16[64,512]{1,0:T(8,128)(2,1)S(1)}, bf16[64,512]{1,0:T(8,128)(2,1)S(1)}, u32[]{:S(2)}, u32[]{:S(2)}) collective-permute-start(bf16[64,512]{1,0:T(8,128)(2,1)S(1)} %convert_multiply_fusion), channel_id=1, source_target_pairs={{32,0},{33,1},{34,2},{35,3},{36,4},{37,5},{38,6},{39,7},{40,8},{41... | collective-permute-start | bytes 196616 | tf_op jit(solution)/shard_map/ppermute | solution.py:18
  9.3 7.6 %collective-permute-start.3 = (bf16[64,512]{1,0:T(8,128)(2,1)S(1)}, bf16[64,512]{1,0:T(8,128)(2,1)S(1)}, u32[]{:S(2)}, u32[]{:S(2)}) collective-permute-start(bf16[64,512]{1,0:T(8,128)(2,1)S(1)} %convert_multiply_fusion), channel_id=1, source_target_pairs={{48,0},{49,1},{50,2},{51,3},{52,4},{53,5},{54,6},{55,7},{56,8},{57... | collective-permute-start | bytes 196616 | tf_op jit(solution)/shard_map/ppermute | solution.py:18
  13.7 0.7 copy-start
  17.7 17.3 %collective-permute-start.6 = (bf16[64,512]{1,0:T(8,128)(2,1)S(1)}, bf16[64,512]{1,0:T(8,128)(2,1)S(1)}, u32[]{:S(2)}, u32[]{:S(2)}) collective-permute-start(bf16[64,512]{1,0:T(8,128)(2,1)S(1)} %bitcast.89), channel_id=1, source_target_pairs={{33,0},{34,1},{35,2},{36,3},{37,4},{38,5},{39,6},{40,7},{41,8},{42... | collective-permute-start | bytes 196616 | tf_op jit(solution)/shard_map/ppermute | solution.py:18
  27.8 7.9 %collective-permute-start.5 = (bf16[64,512]{1,0:T(8,128)(2,1)S(1)}, bf16[64,512]{1,0:T(8,128)(2,1)S(1)}, u32[]{:S(2)}, u32[]{:S(2)}) collective-permute-start(bf16[64,512]{1,0:T(8,128)(2,1)S(1)} %bitcast.90), channel_id=1, source_target_pairs={{17,0},{18,1},{19,2},{20,3},{21,4},{22,5},{23,6},{24,7},{25,8},{26... | collective-permute-start | bytes 196616 | tf_op jit(solution)/shard_map/ppermute | solution.py:18
  29.8 6.6 %collective-permute-start.4 = (bf16[64,512]{1,0:T(8,128)(2,1)S(1)}, bf16[64,512]{1,0:T(8,128)(2,1)S(1)}, u32[]{:S(2)}, u32[]{:S(2)}) collective-permute-start(bf16[64,512]{1,0:T(8,128)(2,1)S(1)} %bitcast.91), channel_id=1, source_target_pairs={{1,0},{2,1},{3,2},{4,3},{5,4},{6,5},{7,6},{8,7},{9,8},{10,9},{11,1... | collective-permute-start | bytes 196616 | tf_op jit(solution)/shard_map/ppermute | solution.py:18
  31.7 7.7 %collective-permute-start.7 = (bf16[64,512]{1,0:T(8,128)(2,1)S(1)}, bf16[64,512]{1,0:T(8,128)(2,1)S(1)}, u32[]{:S(2)}, u32[]{:S(2)}) collective-permute-start(bf16[64,512]{1,0:T(8,128)(2,1)S(1)} %bitcast.92), channel_id=1, source_target_pairs={{49,0},{50,1},{51,2},{52,3},{53,4},{54,5},{55,6},{56,7},{57,8},{58... | collective-permute-start | bytes 196616 | tf_op jit(solution)/shard_map/ppermute | solution.py:18
  40.2 13.7 %collective-permute-start.10 = (bf16[64,512]{1,0:T(8,128)(2,1)S(1)}, bf16[64,512]{1,0:T(8,128)(2,1)S(1)}, u32[]{:S(2)}, u32[]{:S(2)}) collective-permute-start(bf16[64,512]{1,0:T(8,128)(2,1)S(1)} %bitcast.93), channel_id=1, source_target_pairs={{34,0},{35,1},{36,2},{37,3},{38,4},{39,5},{40,6},{41,7},{42,8},{43... | collective-permute-start | bytes 196616 | tf_op jit(solution)/shard_map/ppermute | solution.py:18
  42.2 12.4 %collective-permute-start.9 = (bf16[64,512]{1,0:T(8,128)(2,1)S(1)}, bf16[64,512]{1,0:T(8,128)(2,1)S(1)}, u32[]{:S(2)}, u32[]{:S(2)}) collective-permute-start(bf16[64,512]{1,0:T(8,128)(2,1)S(1)} %bitcast.94), channel_id=1, source_target_pairs={{18,0},{19,1},{20,2},{21,3},{22,4},{23,5},{24,6},{25,7},{26,8},{27... | collective-permute-start | bytes 196616 | tf_op jit(solution)/shard_map/ppermute | solution.py:18
  49.0 6.3 %collective-permute-start.8 = (bf16[64,512]{1,0:T(8,128)(2,1)S(1)}, bf16[64,512]{1,0:T(8,128)(2,1)S(1)}, u32[]{:S(2)}, u32[]{:S(2)}) collective-permute-start(bf16[64,512]{1,0:T(8,128)(2,1)S(1)} %bitcast.95), channel_id=1, source_target_pairs={{2,0},{3,1},{4,2},{5,3},{6,4},{7,5},{8,6},{9,7},{10,8},{11,9},{12,... | collective-permute-start | bytes 196616 | tf_op jit(solution)/shard_map/ppermute | solution.py:18
  52.0 7.8 %collective-permute-start.11 = (bf16[64,512]{1,0:T(8,128)(2,1)S(1)}, bf16[64,512]{1,0:T(8,128)(2,1)S(1)}, u32[]{:S(2)}, u32[]{:S(2)}) collective-permute-start(bf16[64,512]{1,0:T(8,128)(2,1)S(1)} %bitcast.96), channel_id=1, source_target_pairs={{50,0},{51,1},{52,2},{53,3},{54,4},{55,5},{56,6},{57,7},{58,8},{59... | collective-permute-start | bytes 196616 | tf_op jit(solution)/shard_map/ppermute | solution.py:18
where the time goes:
time: 76.8 us; the launch traced here: 76.3 us
  starting transfers between devices  41.1 us (54%)
  blocking collectives  14.3 us (19%)
  local copies, waits for them, and re-layouts  8.59 us (11%)
  waiting for transfers between devices  6.21 us (8%)
  other arithmetic  3.93 us (5%)
  matrix products  1.21 us (2%)
  between operations  0.96 us (1%)
    ppermute x12, starting transfers between devices, from_behind(): return lax.ppermute(block, axis, route)  41.1 us
    all_to_all x1, blocking collectives, sent_and_summed(): lax.all_to_all(in_blocks(array, dim, devices), axis, 0, 0, tiled=True)  14.3 us
    gather x12, local copies, waits for them, and re-layouts, on_device(): jnp.take(arrived, local_rows, axis=0).reshape(blocks_count, IB, columns)  7.08 us
    ppermute x12, waiting for transfers between devices, from_behind(): return lax.ppermute(block, axis, route)  6.21 us
  transfers between devices with their start and end apart: 12, of which 2 were waited for; matrix products, arithmetic and copies ran while one was open for 11% of the time, Pallas kernels for 0%

commit v1 on v0

v1 whole, which is shorter than its diff:
```python
import jax
import jax.numpy as jnp
from jax import lax
from jax.experimental import pallas as pl
from jax.experimental.pallas import tpu as pltpu
from jax.sharding import PartitionSpec as P

KB = 4
IB = 8
OB = 32
LANES = 128

bias_value = 0.35
ceiling = 32.0


def from_ahead(block, axis, distance):
    devices = lax.axis_size(axis)
    route = [((i + distance) % devices, i) for i in range(devices)]
    return lax.ppermute(block, axis, route)


def pack_kernel(values_ref, mask_ref, weights_ref, index_ref, first_ref, second_ref, third_ref):
    rows, columns = values_ref.shape
    outs = weights_ref.shape[-1]
    half = KB * outs
    run_blocks = rows // IB
    first_ref[0:rows, :] = values_ref[...] * mask_ref[...].astype(jnp.float32).astype(jnp.bfloat16)
    block_of_lane = lax.broadcasted_iota(jnp.int32, (IB, half), 1) // OB
    for layer in range(3):
        table = jnp.concatenate([weights_ref[layer, k].astype(jnp.float32) for k in range(KB)], axis=1)
        inner = jnp.zeros((IB, half), jnp.int32)
        for k in range(KB):
            for d in range(outs // OB):
                lane_block = k * (outs // OB) + d
                inner = jnp.where(block_of_lane == lane_block, index_ref[layer, d, k] % run_blocks, inner)
        packed = jnp.concatenate([table, inner.astype(jnp.float32)], axis=1).astype(jnp.bfloat16)
        if layer == 0:
            first_ref[rows : rows + IB, :] = packed
        elif layer == 1:
            second_ref[...] = packed
        else:
            third_ref[...] = packed


def dense_transposed(gathered_ref, table_row, outs, positions, run_blocks):
    half = KB * outs
    tables = [gathered_ref[p, table_row : table_row + IB, :].astype(jnp.float32) for p in range(positions)]
    rows = []
    for source in range(positions):
        w_parts, i_parts = [], []
        for target in range(positions):
            k = (source - target) % positions
            w_parts.append(tables[target][:, k * outs : (k + 1) * outs])
            i_parts.append(tables[target][:, half + k * outs : half + (k + 1) * outs])
        w_row = jnp.concatenate(w_parts, axis=1)
        i_row = jnp.concatenate(i_parts, axis=1)
        for b in range(run_blocks):
            rows.append(jnp.where(i_row == float(b), w_row, 0.0))
    return jnp.concatenate(rows, axis=0).astype(jnp.bfloat16)


def advance(dense_t, activity):
    summed = lax.dot_general(
        dense_t, activity, (((0,), (0,)), ((), ())), preferred_element_type=jnp.float32
    )
    return jnp.minimum(jnp.maximum(summed - bias_value, 0.0), ceiling).astype(jnp.bfloat16)


def layers_kernel(place_ref, gathered_ref, activations_ref, sums_ref, last_ref, totals_ref):
    positions, _, columns = gathered_ref.shape
    rows = activations_ref.shape[0]
    run_blocks = rows // IB
    activity = jnp.concatenate([gathered_ref[p, 0:rows, :] for p in range(positions)], axis=0)
    for layer in range(3):
        dense_t = dense_transposed(gathered_ref, rows + layer * IB, rows, positions, run_blocks)
        activity = advance(dense_t, activity)
    last_ref[...] = activity.reshape(positions, rows, columns)
    activations_ref[...] = last_ref[place_ref[0]]
    totals = jnp.sum(activity.astype(jnp.float32), axis=0, keepdims=True)
    share = columns // positions
    for p in range(positions):
        totals_ref[p] = totals[:, p * share : (p + 1) * share]
    sums_ref[...] = jnp.broadcast_to(totals_ref[place_ref[0]][None], sums_ref.shape)


def on_device(image_values, image_mask, weights, block_index):
    rows, columns = image_values.shape
    devices = lax.axis_size("neu")
    stride = devices // KB
    layer_count = weights.shape[0]
    vmem = pl.BlockSpec(memory_space=pltpu.VMEM)
    smem = pl.BlockSpec(memory_space=pltpu.SMEM)
    first, second, third = pl.pallas_call(
        pack_kernel,
        in_specs=[vmem, vmem, vmem, smem],
        out_specs=[vmem, vmem, vmem],
        out_shape=[
            jax.ShapeDtypeStruct((rows + IB, columns), jnp.bfloat16),
            jax.ShapeDtypeStruct((IB, columns), jnp.bfloat16),
            jax.ShapeDtypeStruct((IB, columns), jnp.bfloat16),
        ],
        name="pack",
    )(image_values, image_mask, weights.transpose(0, 2, 3, 1), block_index)
    first = from_ahead(first, "neu", 3)
    second = from_ahead(second, "neu", 2)
    message = jnp.concatenate([first, second, third], axis=0)
    along_x = [[p * stride + g for p in range(KB)] for g in range(stride)]
    gathered = lax.all_to_all(
        jnp.broadcast_to(message[None], (KB, *message.shape)), "neu", 0, 0, axis_index_groups=along_x, tiled=True
    )
    me = lax.axis_index("neu")
    share = columns // KB
    activations, sums = pl.pallas_call(
        layers_kernel,
        in_specs=[smem, vmem],
        out_specs=[vmem, vmem],
        out_shape=[
            jax.ShapeDtypeStruct((rows, columns), jnp.bfloat16),
            jax.ShapeDtypeStruct((stride, 1, share), jnp.float32),
        ],
        scratch_shapes=[
            pltpu.VMEM((KB, rows, columns), jnp.bfloat16),
            pltpu.VMEM((KB, 1, share), jnp.float32),
        ],
        name="layers",
    )((me // stride).astype(jnp.int32).reshape(1), gathered)
    across = [[p * stride + g for g in range(stride)] for p in range(KB)]
    parts = lax.all_to_all(sums, "neu", 0, 0, axis_index_groups=across, tiled=True)
    own = columns // devices
    totals = lax.dynamic_slice(jnp.sum(parts, axis=(0, 1)), ((me % stride) * own,), (own,))
    return activations, totals


def solution(mesh):
    in_specs = (P("neu", "img"), P("neu", "img"), P(None, "neu", None, None), P(None, "neu", None))
    out_specs = (P("neu", "img"), P(("img", "neu")))
    return jax.shard_map(
        on_device, mesh=mesh, in_specs=in_specs, out_specs=out_specs, check_vma=False
    )
```

time: 76.8 us -> 44.9 us (0.58)
  starting transfers between devices: 41.1 us -> 22.4 us
  blocking collectives: 14.3 us -> 0 us
  waiting for transfers between devices: 6.21 us -> 14.7 us
  local copies, waits for them, and re-layouts: 8.59 us -> 2.09 us
  Pallas kernels: 0 us -> 3.99 us
  other arithmetic: 3.93 us -> 0.74 us
  matrix products: 1.21 us -> 0 us
    ppermute x12 -> x2, starting transfers between devices: 41.1 us -> 11.6 us  [from_ahead(): return lax.ppermute(block, axis, route)]
    all_to_all x1 -> x0, blocking collectives: 14.3 us -> none  [sent_and_summed(): lax.all_to_all(in_blocks(array, dim, devices), axis, 0, 0, tiled=True)]
    all_to_all x0 -> x2, waiting for transfers between devices: none -> 13 us  [the longest x1 7.04 us: on_device(): lax.all_to_all(sums, 'neu', 0, 0, axis_index_groups=across, tiled=True)]
    all_to_all x0 -> x2, starting transfers between devices: none -> 10.7 us  [the longest x1 7.27 us: on_device(): lax.all_to_all(sums, 'neu', 0, 0, axis_index_groups=across, tiled=True)]
    gather x12 -> x0, local copies, waits for them, and re-layouts: 7.08 us -> none  [on_device(): jnp.take(arrived, local_rows, axis=0).reshape(blocks_count, IB, columns)]
    ppermute x12 -> x2, waiting for transfers between devices: 6.21 us -> 1.63 us  [from_ahead(): return lax.ppermute(block, axis, route)]
    pallas_call x0 -> x2, Pallas kernels: none -> 3.99 us  [the longest x1 2.36 us: on_device(): pl.pallas_call(layers_kernel, in_specs=[smem, vmem], out_specs=[vmem, vme...]
    mul x3 -> x0, other arithmetic: 1.48 us -> none  [the longest x1 0.96 us: on_device(): activity = image_values * image_mask.astype(jnp.bfloat16)]
  transfers between devices with their start and end apart: 12 -> 4, of which waited for: 2 -> 3; matrix products, arithmetic and copies ran while one was open for 11% -> 0% of each run, Pallas kernels for 0% -> 0%
where the time goes in v1:
time: 44.9 us; the launch traced here: 44.5 us
  starting transfers between devices  22.4 us (50%)
  waiting for transfers between devices  14.7 us (33%)
  Pallas kernels  3.99 us (9%)
  local copies, waits for them, and re-layouts  2.09 us (5%)
  other arithmetic  0.74 us (2%)
  between operations  0.68 us (2%)
    ppermute x2, starting transfers between devices, from_ahead(): return lax.ppermute(block, axis, route)  11.6 us
    all_to_all x1, starting transfers between devices, on_device(): lax.all_to_all(sums, 'neu', 0, 0, axis_index_groups=across, tiled=True)  7.27 us
    all_to_all x1, waiting for transfers between devices, on_device(): lax.all_to_all(sums, 'neu', 0, 0, axis_index_groups=across, tiled=True)  7.04 us
    all_to_all x1, waiting for transfers between devices, on_device(): lax.all_to_all(jnp.broadcast_to(message[None], (KB, *message.shape)), 'ne...  6 us
    all_to_all x1, starting transfers between devices, on_device(): lax.all_to_all(jnp.broadcast_to(message[None], (KB, *message.shape)), 'ne...  3.46 us
    pallas_call x1, Pallas kernels, on_device(): pl.pallas_call(layers_kernel, in_specs=[smem, vmem], out_specs=[vmem, vme...  2.36 us
    ppermute x2, waiting for transfers between devices, from_ahead(): return lax.ppermute(block, axis, route)  1.63 us
    pallas_call x1, Pallas kernels, on_device(): pl.pallas_call(pack_kernel, in_specs=[vmem, vmem, vmem, smem], out_specs=...  1.62 us
  transfers between devices with their start and end apart: 4, of which 3 were waited for; matrix products, arithmetic and copies ran while one was open for 0% of the time, Pallas kernels for 0%

profile of v1, /device:TPU:1, one launch (start us, length us, event | category | flops | bytes accessed | tf_op | source)
XLA Modules:
  0.0 44.5 jit_solution(6164334005352118353)
XLA Ops:
  0.6 1.6 %pack.1 = (bf16[72,512]{1,0:T(8,128)(2,1)}, bf16[8,512]{1,0:T(8,128)(2,1)}, bf16[8,512]{1,0:T(8,128)(2,1)}) custom-call(bf16[64,512]{1,0:T(8,128)(2,1)} %values_ref.1, s32[64,512]{1,0:T(8,128)} %mask_ref.1, bf16[3,4,8,64]{3,2,1,0:T(8,128)(2,1)} %bitcast.2, s32[3,2,4]{2,1,0:T(2,128)} %index_ref.1), custom_call_target="tpu_custom_call" | custom-call | tf_op jit(solution)/shard_map/pack/pallas_call | solution.py:94
  2.3 8.7 %collective-permute-start = (bf16[72,512]{1,0:T(8,128)(2,1)}, bf16[72,512]{1,0:T(8,128)(2,1)S(1)}, u32[]{:S(2)}, u32[]{:S(2)}) collective-permute-start(bf16[72,512]{1,0:T(8,128)(2,1)} %get-tuple-element.7), channel_id=1, source_target_pairs={{3,0},{4,1},{5,2},{6,3},{7,4},{8,5},{9,6},{10,7},{11,8},{12,9},{13... | collective-permute-start | bytes 221192 | tf_op jit(solution)/shard_map/ppermute | solution.py:20
  10.9 3.0 %collective-permute-start.1 = (bf16[8,512]{1,0:T(8,128)(2,1)}, bf16[8,512]{1,0:T(8,128)(2,1)S(1)}, u32[]{:S(2)}, u32[]{:S(2)}) collective-permute-start(bf16[8,512]{1,0:T(8,128)(2,1)} %get-tuple-element.8), channel_id=1, source_target_pairs={{2,0},{3,1},{4,2},{5,3},{6,4},{7,5},{8,6},{9,7},{10,8},{11,9},{12,... | collective-permute-start | bytes 24584 | tf_op jit(solution)/shard_map/ppermute | solution.py:20
  13.9 1.6 %collective-permute-done.1 = bf16[8,512]{1,0:T(8,128)(2,1)S(1)} collective-permute-done((bf16[8,512]{1,0:T(8,128)(2,1)}, bf16[8,512]{1,0:T(8,128)(2,1)S(1)}, u32[]{:S(2)}, u32[]{:S(2)}) %collective-permute-start.1) | collective-permute-done | bytes 8224 | tf_op jit(solution)/shard_map/ppermute | solution.py:20
  15.5 0.0 collective-permute-done
  15.5 0.7 %pad_maximum_fusion = bf16[88,512]{1,0:T(8,128)(2,1)S(1)} fusion(bf16[8,512]{1,0:T(8,128)(2,1)} %get-tuple-element.9, bf16[8,512]{1,0:T(8,128)(2,1)S(1)} %collective-permute-done.1, bf16[72,512]{1,0:T(8,128)(2,1)S(1)} %collective-permute-done), kind=kLoop, calls=%fused_computation | loop fusion | flops 270336 | bytes 180224 | tf_op jit(solution)/shard_map/concatenate | solution.py:107
  16.2 0.8 %broadcast_in_dim.2 = bf16[4,88,512]{2,1,0:T(8,128)(2,1)} broadcast(bf16[88,512]{1,0:T(8,128)(2,1)S(1)} %pad_maximum_fusion), dimensions={1,2} | broadcast | bytes 450560 | tf_op jit(solution)/shard_map/broadcast_in_dim | solution.py:110
  17.0 3.5 %all-to-all-start = ((bf16[4,88,512]{2,1,0:T(8,128)(2,1)}), bf16[4,88,512]{2,1,0:T(8,128)(2,1)S(1)}, u32[]{:S(2)}, u32[]{:S(2)}) async-start(bf16[4,88,512]{2,1,0:T(8,128)(2,1)} %broadcast_in_dim.2), calls=%async_computation | async-start | bytes 720896 | tf_op jit(solution)/shard_map/all_to_all | solution.py:109
  20.5 6.0 %all-to-all-done.gathered_ref = bf16[4,88,512]{2,1,0:T(8,128)(2,1)S(1)} async-done(((bf16[4,88,512]{2,1,0:T(8,128)(2,1)}), bf16[4,88,512]{2,1,0:T(8,128)(2,1)S(1)}, u32[]{:S(2)}, u32[]{:S(2)}) %all-to-all-start) | async-done | bytes 360480 | tf_op jit(solution)/shard_map/all_to_all | solution.py:109
  26.5 0.0 copy-start
  26.5 0.7 %copy-done = bf16[4,88,512]{2,1,0:T(8,128)(2,1)} copy-done((bf16[4,88,512]{2,1,0:T(8,128)(2,1)}, bf16[4,88,512]{2,1,0:T(8,128)(2,1)S(1)}, u32[]{:S(2)}) %copy-start) | copy-done | bytes 360472
  27.2 2.4 %layers.1 = (bf16[64,512]{1,0:T(8,128)(2,1)}, f32[16,1,128]{2,1,0:T(1,128)}) custom-call(s32[1]{0:T(128)} %bitcast.place_ref, bf16[4,88,512]{2,1,0:T(8,128)(2,1)} %copy-done), custom_call_target="tpu_custom_call" | custom-call | tf_op jit(solution)/shard_map/layers/pallas_call | solution.py:114
  29.6 7.3 %all-to-all-start.1 = ((f32[16,1,128]{2,1,0:T(1,128)}), f32[16,1,128]{2,1,0:T(1,128)S(1)}, u32[]{:S(2)}, u32[]{:S(2)}) async-start(f32[16,1,128]{2,1,0:T(1,128)} %get-tuple-element.11), calls=%async_computation.1 | async-start | bytes 16384 | tf_op jit(solution)/shard_map/all_to_all | solution.py:129
  36.9 7.0 %all-to-all-done.1 = f32[16,1,128]{2,1,0:T(1,128)S(1)} async-done(((f32[16,1,128]{2,1,0:T(1,128)}), f32[16,1,128]{2,1,0:T(1,128)S(1)}, u32[]{:S(2)}, u32[]{:S(2)}) %all-to-all-start.1) | async-done | bytes 8224 | tf_op jit(solution)/shard_map/all_to_all | solution.py:129
  43.9 0.6 %dynamic_slice.3 = f32[8]{0:T(128)} dynamic-slice(f32[128]{0:T(128)S(1)} %reduce_sum.9, s32[]{:T(128)S(6)} %select_n.16), dynamic_slice_sizes={8} | dynamic-slice | bytes 68 | tf_op jit(solution)/shard_map/dynamic_slice | solution.py:131
  (1 shorter events, 0.0 us)
Async XLA Ops:
  2.3 13.3 %collective-permute-start = (bf16[72,512]{1,0:T(8,128)(2,1)}, bf16[72,512]{1,0:T(8,128)(2,1)S(1)}, u32[]{:S(2)}, u32[]{:S(2)}) collective-permute-start(bf16[72,512]{1,0:T(8,128)(2,1)} %get-tuple-element.7), channel_id=1, source_target_pairs={{3,0},{4,1},{5,2},{6,3},{7,4},{8,5},{9,6},{10,7},{11,8},{12,9},{13... | collective-permute-start | bytes 221192 | tf_op jit(solution)/shard_map/ppermute | solution.py:20
  10.9 4.6 %collective-permute-start.1 = (bf16[8,512]{1,0:T(8,128)(2,1)}, bf16[8,512]{1,0:T(8,128)(2,1)S(1)}, u32[]{:S(2)}, u32[]{:S(2)}) collective-permute-start(bf16[8,512]{1,0:T(8,128)(2,1)} %get-tuple-element.8), channel_id=1, source_target_pairs={{2,0},{3,1},{4,2},{5,3},{6,4},{7,5},{8,6},{9,7},{10,8},{11,9},{12,... | collective-permute-start | bytes 24584 | tf_op jit(solution)/shard_map/ppermute | solution.py:20
  17.0 9.5 %all-to-all-start = ((bf16[4,88,512]{2,1,0:T(8,128)(2,1)}), bf16[4,88,512]{2,1,0:T(8,128)(2,1)S(1)}, u32[]{:S(2)}, u32[]{:S(2)}) async-start(bf16[4,88,512]{2,1,0:T(8,128)(2,1)} %broadcast_in_dim.2), calls=%async_computation | async-start | bytes 720896 | tf_op jit(solution)/shard_map/all_to_all | solution.py:109
  26.5 0.7 %copy-start = (bf16[4,88,512]{2,1,0:T(8,128)(2,1)}, bf16[4,88,512]{2,1,0:T(8,128)(2,1)S(1)}, u32[]{:S(2)}) copy-start(bf16[4,88,512]{2,1,0:T(8,128)(2,1)S(1)} %all-to-all-done.gathered_ref) | copy-start | bytes 1081348
  29.6 14.3 %all-to-all-start.1 = ((f32[16,1,128]{2,1,0:T(1,128)}), f32[16,1,128]{2,1,0:T(1,128)S(1)}, u32[]{:S(2)}, u32[]{:S(2)}) async-start(f32[16,1,128]{2,1,0:T(1,128)} %get-tuple-element.11), calls=%async_computation.1 | async-start | bytes 16384 | tf_op jit(solution)/shard_map/all_to_all | solution.py:129

commit v2 on v1

--- a/solution.py
+++ b/solution.py
@@ -96,12 +96,15 @@
         in_specs=[vmem, vmem, vmem, smem],
         out_specs=[vmem, vmem, vmem],
         out_shape=[
-            jax.ShapeDtypeStruct((rows + IB, columns), jnp.bfloat16),
-            jax.ShapeDtypeStruct((IB, columns), jnp.bfloat16),
-            jax.ShapeDtypeStruct((IB, columns), jnp.bfloat16),
+            pltpu.VMEM((rows + IB, columns), jnp.bfloat16),
+            pltpu.VMEM((IB, columns), jnp.bfloat16),
+            pltpu.VMEM((IB, columns), jnp.bfloat16),
         ],
         name="pack",
     )(image_values, image_mask, weights.transpose(0, 2, 3, 1), block_index)
+    me = lax.axis_index("neu")
+    place, begin = me // stride, (me % stride) * (columns // devices)
+    first, place, begin = lax.optimization_barrier((first, place, begin))
     first = from_ahead(first, "neu", 3)
     second = from_ahead(second, "neu", 2)
     message = jnp.concatenate([first, second, third], axis=0)
@@ -109,7 +112,6 @@
     gathered = lax.all_to_all(
         jnp.broadcast_to(message[None], (KB, *message.shape)), "neu", 0, 0, axis_index_groups=along_x, tiled=True
     )
-    me = lax.axis_index("neu")
     share = columns // KB
     activations, sums = pl.pallas_call(
         layers_kernel,
@@ -117,18 +119,18 @@
         out_specs=[vmem, vmem],
         out_shape=[
             jax.ShapeDtypeStruct((rows, columns), jnp.bfloat16),
-            jax.ShapeDtypeStruct((stride, 1, share), jnp.float32),
+            pltpu.VMEM((stride, 1, share), jnp.float32),
         ],
         scratch_shapes=[
             pltpu.VMEM((KB, rows, columns), jnp.bfloat16),
             pltpu.VMEM((KB, 1, share), jnp.float32),
         ],
         name="layers",
-    )((me // stride).astype(jnp.int32).reshape(1), gathered)
+    )(place.reshape(1), pltpu.with_memory_space_constraint(gathered, pltpu.VMEM))
     across = [[p * stride + g for g in range(stride)] for p in range(KB)]
     parts = lax.all_to_all(sums, "neu", 0, 0, axis_index_groups=across, tiled=True)
     own = columns // devices
-    totals = lax.dynamic_slice(jnp.sum(parts, axis=(0, 1)), ((me % stride) * own,), (own,))
+    totals = lax.dynamic_slice(jnp.sum(parts, axis=(0, 1)), (begin,), (own,))
     return activations, totals
 
 

time: 44.9 us -> 40.6 us (0.904)
  blocking collectives: 0 us -> 8.44 us
  waiting for transfers between devices: 14.7 us -> 8.44 us
  starting transfers between devices: 22.4 us -> 19.8 us
  Pallas kernels: 3.99 us -> 2.38 us
  local copies, waits for them, and re-layouts: 2.09 us -> 0.61 us
  other arithmetic: 0.74 us -> 0.04 us
    all_to_all x0 -> x1, blocking collectives: none -> 8.44 us  [on_device(): lax.all_to_all(jnp.broadcast_to(message[None], (KB, *message.shape)), 'ne...]
    all_to_all x1 -> x0, waiting for transfers between devices: 6 us -> none  [on_device(): lax.all_to_all(jnp.broadcast_to(message[None], (KB, *message.shape)), 'ne...]
    all_to_all x1 -> x0, starting transfers between devices: 3.46 us -> none  [on_device(): lax.all_to_all(jnp.broadcast_to(message[None], (KB, *message.shape)), 'ne...]
    pallas_call x1, Pallas kernels: 2.36 us -> 1.38 us  [on_device(): pl.pallas_call(layers_kernel, in_specs=[smem, vmem], out_specs=[vmem, vme...]
    all_to_all x1, starting transfers between devices: 7.27 us -> 8.13 us  [on_device(): lax.all_to_all(sums, 'neu', 0, 0, axis_index_groups=across, tiled=True)]
    unnamed x2 -> x0, local copies, waits for them, and re-layouts: 0.74 us -> none
    broadcast_in_dim x1, local copies, waits for them, and re-layouts: 0.76 us -> 0.03 us  [on_device(): jnp.broadcast_to(message[None], (KB, *message.shape))]
    concatenate x1, other arithmetic: 0.7 us -> 0.01 us  [on_device(): message = jnp.concatenate([first, second, third], axis=0)]
  transfers between devices with their start and end apart: 4 -> 3, of which waited for: 3 -> 2; matrix products, arithmetic and copies ran while one was open for 0% -> 0% of each run, Pallas kernels for 0% -> 0%
where the time goes in v2:
time: 40.6 us; the launch traced here: 40.4 us
  starting transfers between devices  19.8 us (49%)
  waiting for transfers between devices  8.44 us (21%)
  blocking collectives  8.44 us (21%)
  Pallas kernels  2.38 us (6%)
  between operations  0.68 us (2%)
  local copies, waits for them, and re-layouts  0.61 us (2%)
    ppermute x2, starting transfers between devices, from_ahead(): return lax.ppermute(block, axis, route)  11.7 us
    all_to_all x1, blocking collectives, on_device(): lax.all_to_all(jnp.broadcast_to(message[None], (KB, *message.shape)), 'ne...  8.44 us
    all_to_all x1, starting transfers between devices, on_device(): lax.all_to_all(sums, 'neu', 0, 0, axis_index_groups=across, tiled=True)  8.13 us
    all_to_all x1, waiting for transfers between devices, on_device(): lax.all_to_all(sums, 'neu', 0, 0, axis_index_groups=across, tiled=True)  7.03 us
    ppermute x2, waiting for transfers between devices, from_ahead(): return lax.ppermute(block, axis, route)  1.42 us
    pallas_call x1, Pallas kernels, on_device(): pl.pallas_call(layers_kernel, in_specs=[smem, vmem], out_specs=[vmem, vme...  1.38 us
    pallas_call x1, Pallas kernels, on_device(): pl.pallas_call(pack_kernel, in_specs=[vmem, vmem, vmem, smem], out_specs=...  1 us
  transfers between devices with their start and end apart: 3, of which 2 were waited for; matrix products, arithmetic and copies ran while one was open for 0% of the time, Pallas kernels for 0%

profile of v2, /device:TPU:1, one launch (start us, length us, event | category | flops | bytes accessed | tf_op | source)
XLA Modules:
  0.0 40.4 jit_solution(1115178724397144078)
XLA Ops:
  0.7 1.0 %pack.1 = (bf16[72,512]{1,0:T(8,128)(2,1)S(1)}, bf16[8,512]{1,0:T(8,128)(2,1)S(1)}, bf16[8,512]{1,0:T(8,128)(2,1)S(1)}) custom-call(bf16[64,512]{1,0:T(8,128)(2,1)} %values_ref.1, s32[64,512]{1,0:T(8,128)} %mask_ref.1, bf16[3,4,8,64]{3,2,1,0:T(8,128)(2,1)} %bitcast.2, s32[3,2,4]{2,1,0:T(2,128)} %index_ref.1), custom_call_target="tpu_custom_call" | custom-call | tf_op jit(solution)/shard_map/pack/pallas_call | solution.py:94
  1.6 8.7 %collective-permute-start = (bf16[72,512]{1,0:T(8,128)(2,1)S(1)}, bf16[72,512]{1,0:T(8,128)(2,1)S(1)}, u32[]{:S(2)}, u32[]{:S(2)}) collective-permute-start(bf16[72,512]{1,0:T(8,128)(2,1)S(1)} %get-tuple-element.12), channel_id=1, source_target_pairs={{3,0},{4,1},{5,2},{6,3},{7,4},{8,5},{9,6},{10,7},{11,8},{12,9},{13... | collective-permute-start | bytes 221192 | tf_op jit(solution)/shard_map/ppermute | solution.py:20
  10.3 3.0 %collective-permute-start.1 = (bf16[8,512]{1,0:T(8,128)(2,1)S(1)}, bf16[8,512]{1,0:T(8,128)(2,1)S(1)}, u32[]{:S(2)}, u32[]{:S(2)}) collective-permute-start(bf16[8,512]{1,0:T(8,128)(2,1)S(1)} %get-tuple-element.13), channel_id=1, source_target_pairs={{2,0},{3,1},{4,2},{5,3},{6,4},{7,5},{8,6},{9,7},{10,8},{11,9},{12,... | collective-permute-start | bytes 24584 | tf_op jit(solution)/shard_map/ppermute | solution.py:20
  13.3 1.4 %collective-permute-done.1 = bf16[8,512]{1,0:T(8,128)(2,1)S(1)} collective-permute-done((bf16[8,512]{1,0:T(8,128)(2,1)S(1)}, bf16[8,512]{1,0:T(8,128)(2,1)S(1)}, u32[]{:S(2)}, u32[]{:S(2)}) %collective-permute-start.1) | collective-permute-done | bytes 8224 | tf_op jit(solution)/shard_map/ppermute | solution.py:20
  14.7 0.0 collective-permute-done
  14.8 8.4 %all_to_all.10.gathered_ref = bf16[4,88,512]{2,1,0:T(8,128)(2,1)S(1)} all-to-all(bf16[4,88,512]{2,1,0:T(8,128)(2,1)S(1)} %broadcast_in_dim.2), channel_id=1, replica_groups={{0,16,32,48},{1,17,33,49},{2,18,34,50},{3,19,35,51},{4,20,36,52},{5,21,..., dimensions={0} | all-to-all | bytes 720896 | tf_op jit(solution)/shard_map/all_to_all | solution.py:112
  23.2 1.4 %layers.1 = (bf16[64,512]{1,0:T(8,128)(2,1)}, f32[16,1,128]{2,1,0:T(1,128)}) custom-call(s32[1]{0:T(128)} %bitcast.1.place_ref, bf16[4,88,512]{2,1,0:T(8,128)(2,1)S(1)} %all_to_all.10.gathered_ref), custom_call_target="tpu_custom_call" | custom-call | tf_op jit(solution)/shard_map/layers/pallas_call | solution.py:116
  24.6 8.1 %all-to-all-start.1 = ((f32[16,1,128]{2,1,0:T(1,128)}), f32[16,1,128]{2,1,0:T(1,128)S(1)}, u32[]{:S(2)}, u32[]{:S(2)}) async-start(f32[16,1,128]{2,1,0:T(1,128)} %get-tuple-element.16), calls=%async_computation.1 | async-start | bytes 16384 | tf_op jit(solution)/shard_map/all_to_all | solution.py:131
  32.7 7.0 %all-to-all-done.1 = f32[16,1,128]{2,1,0:T(1,128)S(1)} async-done(((f32[16,1,128]{2,1,0:T(1,128)}), f32[16,1,128]{2,1,0:T(1,128)S(1)}, u32[]{:S(2)}, u32[]{:S(2)}) %all-to-all-start.1) | async-done | bytes 8224 | tf_op jit(solution)/shard_map/all_to_all | solution.py:131
  39.8 0.6 %dynamic_slice.3 = f32[8]{0:T(128)} dynamic-slice(f32[128]{0:T(128)S(1)} %reduce_sum.9, s32[]{:T(128)S(6)} %select_n.16), dynamic_slice_sizes={8} | dynamic-slice | bytes 68 | tf_op jit(solution)/shard_map/dynamic_slice | solution.py:133
  (3 shorter events, 0.1 us)
Async XLA Ops:
  1.6 13.1 %collective-permute-start = (bf16[72,512]{1,0:T(8,128)(2,1)S(1)}, bf16[72,512]{1,0:T(8,128)(2,1)S(1)}, u32[]{:S(2)}, u32[]{:S(2)}) collective-permute-start(bf16[72,512]{1,0:T(8,128)(2,1)S(1)} %get-tuple-element.12), channel_id=1, source_target_pairs={{3,0},{4,1},{5,2},{6,3},{7,4},{8,5},{9,6},{10,7},{11,8},{12,9},{13... | collective-permute-start | bytes 221192 | tf_op jit(solution)/shard_map/ppermute | solution.py:20
  10.3 4.4 %collective-permute-start.1 = (bf16[8,512]{1,0:T(8,128)(2,1)S(1)}, bf16[8,512]{1,0:T(8,128)(2,1)S(1)}, u32[]{:S(2)}, u32[]{:S(2)}) collective-permute-start(bf16[8,512]{1,0:T(8,128)(2,1)S(1)} %get-tuple-element.13), channel_id=1, source_target_pairs={{2,0},{3,1},{4,2},{5,3},{6,4},{7,5},{8,6},{9,7},{10,8},{11,9},{12,... | collective-permute-start | bytes 24584 | tf_op jit(solution)/shard_map/ppermute | solution.py:20
  24.6 15.2 %all-to-all-start.1 = ((f32[16,1,128]{2,1,0:T(1,128)}), f32[16,1,128]{2,1,0:T(1,128)S(1)}, u32[]{:S(2)}, u32[]{:S(2)}) async-start(f32[16,1,128]{2,1,0:T(1,128)} %get-tuple-element.16), calls=%async_computation.1 | async-start | bytes 16384 | tf_op jit(solution)/shard_map/all_to_all | solution.py:131

commit v3 on v2

--- a/solution.py
+++ b/solution.py
@@ -67,21 +67,36 @@
     return jnp.minimum(jnp.maximum(summed - bias_value, 0.0), ceiling).astype(jnp.bfloat16)
 
 
-def layers_kernel(place_ref, gathered_ref, activations_ref, sums_ref, last_ref, totals_ref):
+def layers_kernel(gathered_ref, activations_ref, sums_ref, last_ref, totals_ref):
     positions, _, columns = gathered_ref.shape
     rows = activations_ref.shape[0]
     run_blocks = rows // IB
+    place = lax.axis_index("neu") // (lax.axis_size("neu") // KB)
     activity = jnp.concatenate([gathered_ref[p, 0:rows, :] for p in range(positions)], axis=0)
     for layer in range(3):
         dense_t = dense_transposed(gathered_ref, rows + layer * IB, rows, positions, run_blocks)
         activity = advance(dense_t, activity)
     last_ref[...] = activity.reshape(positions, rows, columns)
-    activations_ref[...] = last_ref[place_ref[0]]
+    activations_ref[...] = last_ref[place]
     totals = jnp.sum(activity.astype(jnp.float32), axis=0, keepdims=True)
     share = columns // positions
     for p in range(positions):
         totals_ref[p] = totals[:, p * share : (p + 1) * share]
-    sums_ref[...] = jnp.broadcast_to(totals_ref[place_ref[0]][None], sums_ref.shape)
+    sums_ref[...] = jnp.broadcast_to(totals_ref[place][None], sums_ref.shape)
+
+
+def finish_kernel(parts_ref, run_ref, activations_ref, totals_ref, own_ref, copied, summed):
+    out = pltpu.make_async_copy(run_ref, activations_ref, copied)
+    out.start()
+    share = parts_ref.shape[-1]
+    own = totals_ref.shape[-1]
+    begin = (lax.axis_index("neu") % parts_ref.shape[0]) * own
+    totals = jnp.broadcast_to(jnp.sum(parts_ref[...], axis=0), (8, share))
+    own_ref[...] = pltpu.roll(totals, share - begin, 1)[0:1, 0:own]
+    own_out = pltpu.make_async_copy(own_ref, totals_ref, summed)
+    own_out.start()
+    out.wait()
+    own_out.wait()
 
 
 def on_device(image_values, image_mask, weights, block_index):
@@ -102,9 +117,6 @@
         ],
         name="pack",
     )(image_values, image_mask, weights.transpose(0, 2, 3, 1), block_index)
-    me = lax.axis_index("neu")
-    place, begin = me // stride, (me % stride) * (columns // devices)
-    first, place, begin = lax.optimization_barrier((first, place, begin))
     first = from_ahead(first, "neu", 3)
     second = from_ahead(second, "neu", 2)
     message = jnp.concatenate([first, second, third], axis=0)
@@ -115,10 +127,10 @@
     share = columns // KB
     activations, sums = pl.pallas_call(
         layers_kernel,
-        in_specs=[smem, vmem],
+        in_specs=[vmem],
         out_specs=[vmem, vmem],
         out_shape=[
-            jax.ShapeDtypeStruct((rows, columns), jnp.bfloat16),
+            pltpu.VMEM((rows, columns), jnp.bfloat16),
             pltpu.VMEM((stride, 1, share), jnp.float32),
         ],
         scratch_shapes=[
@@ -126,12 +138,28 @@
             pltpu.VMEM((KB, 1, share), jnp.float32),
         ],
         name="layers",
-    )(place.reshape(1), pltpu.with_memory_space_constraint(gathered, pltpu.VMEM))
+    )(pltpu.with_memory_space_constraint(gathered, pltpu.VMEM))
     across = [[p * stride + g for g in range(stride)] for p in range(KB)]
     parts = lax.all_to_all(sums, "neu", 0, 0, axis_index_groups=across, tiled=True)
-    own = columns // devices
-    totals = lax.dynamic_slice(jnp.sum(parts, axis=(0, 1)), (begin,), (own,))
-    return activations, totals
+    activations, totals = pl.pallas_call(
+        finish_kernel,
+        in_specs=[vmem, vmem],
+        out_specs=[pl.BlockSpec(memory_space=pl.ANY)] * 2,
+        out_shape=[
+            jax.ShapeDtypeStruct((rows, columns), jnp.bfloat16),
+            jax.ShapeDtypeStruct((1, columns // devices), jnp.float32),
+        ],
+        scratch_shapes=[
+            pltpu.VMEM((1, columns // devices), jnp.float32),
+            pltpu.SemaphoreType.DMA(()),
+            pltpu.SemaphoreType.DMA(()),
+        ],
+        name="finish",
+    )(
+        pltpu.with_memory_space_constraint(parts, pltpu.VMEM),
+        pltpu.with_memory_space_constraint(activations, pltpu.VMEM),
+    )
+    return activations, totals.reshape(-1)
 
 
 def solution(mesh):

time: 40.6 us -> 39.8 us (0.980)
  blocking collectives: 8.44 us -> 23.4 us
  starting transfers between devices: 19.8 us -> 11.7 us
  waiting for transfers between devices: 8.44 us -> 1.42 us
  local copies, waits for them, and re-layouts: 0.61 us -> 0.03 us
    all_to_all x0 -> x1, blocking collectives: none -> 14.9 us  [on_device(): lax.all_to_all(sums, 'neu', 0, 0, axis_index_groups=across, tiled=True)]
    all_to_all x1 -> x0, starting transfers between devices: 8.13 us -> none  [on_device(): lax.all_to_all(sums, 'neu', 0, 0, axis_index_groups=across, tiled=True)]
    all_to_all x1 -> x0, waiting for transfers between devices: 7.03 us -> none  [on_device(): lax.all_to_all(sums, 'neu', 0, 0, axis_index_groups=across, tiled=True)]
    dynamic_slice x1 -> x0, local copies, waits for them, and re-layouts: 0.59 us -> none  [on_device(): totals = lax.dynamic_slice(jnp.sum(parts, axis=(0, 1)), (begin,), (own,))]
    pallas_call x1 -> x2, Pallas kernels: 1.38 us -> 1.41 us  [the longest x1 0.75 us: on_device(): pl.pallas_call(layers_kernel, in_specs=[vmem], out_specs=[vmem, vmem], ou...]
  transfers between devices with their start and end apart: 3 -> 2, of which waited for: 2 -> 1; matrix products, arithmetic and copies ran while one was open for 0% -> 0% of each run, Pallas kernels for 0% -> 0%
where the time goes in v3:
time: 39.8 us; the launch traced here: 39.5 us
  blocking collectives  23.4 us (59%)
  starting transfers between devices  11.7 us (29%)
  Pallas kernels  2.4 us (6%)
  waiting for transfers between devices  1.42 us (4%)
  between operations  0.67 us (2%)
    all_to_all x1, blocking collectives, on_device(): lax.all_to_all(sums, 'neu', 0, 0, axis_index_groups=across, tiled=True)  14.9 us
    ppermute x2, starting transfers between devices, from_ahead(): return lax.ppermute(block, axis, route)  11.7 us
    all_to_all x1, blocking collectives, on_device(): lax.all_to_all(jnp.broadcast_to(message[None], (KB, *message.shape)), 'ne...  8.44 us
    ppermute x2, waiting for transfers between devices, from_ahead(): return lax.ppermute(block, axis, route)  1.42 us
    pallas_call x1, Pallas kernels, on_device(): pl.pallas_call(pack_kernel, in_specs=[vmem, vmem, vmem, smem], out_specs=...  1 us
  transfers between devices with their start and end apart: 2, of which 1 were waited for; matrix products, arithmetic and copies ran while one was open for 0% of the time, Pallas kernels for 0%

profile of v3, /device:TPU:1, one launch (start us, length us, event | category | flops | bytes accessed | tf_op | source)
XLA Modules:
  0.0 39.5 jit_solution(12028012920843965848)
XLA Ops:
  0.6 1.0 %pack.1 = (bf16[72,512]{1,0:T(8,128)(2,1)S(1)}, bf16[8,512]{1,0:T(8,128)(2,1)S(1)}, bf16[8,512]{1,0:T(8,128)(2,1)S(1)}) custom-call(bf16[64,512]{1,0:T(8,128)(2,1)} %values_ref.1, s32[64,512]{1,0:T(8,128)} %mask_ref.1, bf16[3,4,8,64]{3,2,1,0:T(8,128)(2,1)} %bitcast.2, s32[3,2,4]{2,1,0:T(2,128)} %index_ref.1), custom_call_target="tpu_custom_call" | custom-call | tf_op jit(solution)/shard_map/pack/pallas_call | solution.py:109
  1.6 8.7 %collective-permute-start = (bf16[72,512]{1,0:T(8,128)(2,1)S(1)}, bf16[72,512]{1,0:T(8,128)(2,1)S(1)}, u32[]{:S(2)}, u32[]{:S(2)}) collective-permute-start(bf16[72,512]{1,0:T(8,128)(2,1)S(1)} %get-tuple-element.9), channel_id=1, source_target_pairs={{3,0},{4,1},{5,2},{6,3},{7,4},{8,5},{9,6},{10,7},{11,8},{12,9},{13... | collective-permute-start | bytes 221192 | tf_op jit(solution)/shard_map/ppermute | solution.py:20
  10.3 3.0 %collective-permute-start.1 = (bf16[8,512]{1,0:T(8,128)(2,1)S(1)}, bf16[8,512]{1,0:T(8,128)(2,1)S(1)}, u32[]{:S(2)}, u32[]{:S(2)}) collective-permute-start(bf16[8,512]{1,0:T(8,128)(2,1)S(1)} %get-tuple-element.10), channel_id=1, source_target_pairs={{2,0},{3,1},{4,2},{5,3},{6,4},{7,5},{8,6},{9,7},{10,8},{11,9},{12,... | collective-permute-start | bytes 24584 | tf_op jit(solution)/shard_map/ppermute | solution.py:20
  13.3 1.4 %collective-permute-done.1 = bf16[8,512]{1,0:T(8,128)(2,1)S(1)} collective-permute-done((bf16[8,512]{1,0:T(8,128)(2,1)S(1)}, bf16[8,512]{1,0:T(8,128)(2,1)S(1)}, u32[]{:S(2)}, u32[]{:S(2)}) %collective-permute-start.1) | collective-permute-done | bytes 8224 | tf_op jit(solution)/shard_map/ppermute | solution.py:20
  14.7 0.0 collective-permute-done
  14.8 8.4 %all_to_all.10.gathered_ref = bf16[4,88,512]{2,1,0:T(8,128)(2,1)S(1)} all-to-all(bf16[4,88,512]{2,1,0:T(8,128)(2,1)S(1)} %broadcast_in_dim.2), channel_id=1, replica_groups={{0,16,32,48},{1,17,33,49},{2,18,34,50},{3,19,35,51},{4,20,36,52},{5,21,..., dimensions={0} | all-to-all | bytes 720896 | tf_op jit(solution)/shard_map/all_to_all | solution.py:124
  23.2 0.8 %layers.1 = (bf16[64,512]{1,0:T(8,128)(2,1)S(1)}, f32[16,1,128]{2,1,0:T(1,128)S(1)}) custom-call(bf16[4,88,512]{2,1,0:T(8,128)(2,1)S(1)} %all_to_all.10.gathered_ref), custom_call_target="tpu_custom_call" | custom-call | tf_op jit(solution)/shard_map/layers/pallas_call | solution.py:128
  24.0 14.9 %all_to_all.11.parts_ref = f32[16,1,128]{2,1,0:T(1,128)S(1)} all-to-all(f32[16,1,128]{2,1,0:T(1,128)S(1)} %get-tuple-element.12), channel_id=1, replica_groups={{0,1,2,3,4,5,6,7,8,9,10,11,12,13,14,15},{16,17,18,19,20,21,22,23,24,25,..., dimensions={0} | all-to-all | bytes 16384 | tf_op jit(solution)/shard_map/all_to_all | solution.py:143
  38.9 0.7 %finish.1 = (bf16[64,512]{1,0:T(8,128)(2,1)}, f32[1,8]{1,0:T(1,128)}) custom-call(f32[16,1,128]{2,1,0:T(1,128)S(1)} %all_to_all.11.parts_ref, bf16[64,512]{1,0:T(8,128)(2,1)S(1)} %get-tuple-element.13.run_ref), custom_call_target="tpu_custom_call" | custom-call | tf_op jit(solution)/shard_map/finish/pallas_call | solution.py:144
  (2 shorter events, 0.0 us)
Async XLA Ops:
  1.6 13.1 %collective-permute-start = (bf16[72,512]{1,0:T(8,128)(2,1)S(1)}, bf16[72,512]{1,0:T(8,128)(2,1)S(1)}, u32[]{:S(2)}, u32[]{:S(2)}) collective-permute-start(bf16[72,512]{1,0:T(8,128)(2,1)S(1)} %get-tuple-element.9), channel_id=1, source_target_pairs={{3,0},{4,1},{5,2},{6,3},{7,4},{8,5},{9,6},{10,7},{11,8},{12,9},{13... | collective-permute-start | bytes 221192 | tf_op jit(solution)/shard_map/ppermute | solution.py:20
  10.3 4.4 %collective-permute-start.1 = (bf16[8,512]{1,0:T(8,128)(2,1)S(1)}, bf16[8,512]{1,0:T(8,128)(2,1)S(1)}, u32[]{:S(2)}, u32[]{:S(2)}) collective-permute-start(bf16[8,512]{1,0:T(8,128)(2,1)S(1)} %get-tuple-element.10), channel_id=1, source_target_pairs={{2,0},{3,1},{4,2},{5,3},{6,4},{7,5},{8,6},{9,7},{10,8},{11,9},{12,... | collective-permute-start | bytes 24584 | tf_op jit(solution)/shard_map/ppermute | solution.py:20

commit v4 on v3

--- a/solution.py
+++ b/solution.py
@@ -26,15 +26,19 @@
     half = KB * outs
     run_blocks = rows // IB
     first_ref[0:rows, :] = values_ref[...] * mask_ref[...].astype(jnp.float32).astype(jnp.bfloat16)
-    block_of_lane = lax.broadcasted_iota(jnp.int32, (IB, half), 1) // OB
+    slot = lax.broadcasted_iota(jnp.int32, (IB, LANES), 0)
+    out_block = lax.broadcasted_iota(jnp.int32, (IB, LANES), 1) // OB
+    nothing = jnp.zeros((IB, LANES), jnp.float32)
     for layer in range(3):
         table = jnp.concatenate([weights_ref[layer, k].astype(jnp.float32) for k in range(KB)], axis=1)
-        inner = jnp.zeros((IB, half), jnp.int32)
+        inner = jnp.zeros((IB, LANES), jnp.int32)
         for k in range(KB):
             for d in range(outs // OB):
-                lane_block = k * (outs // OB) + d
-                inner = jnp.where(block_of_lane == lane_block, index_ref[layer, d, k] % run_blocks, inner)
-        packed = jnp.concatenate([table, inner.astype(jnp.float32)], axis=1).astype(jnp.bfloat16)
+                here = (slot == k + (KB if layer == 1 else 0)) & (out_block == d)
+                inner = jnp.where(here, index_ref[layer, d, k] % run_blocks, inner)
+        inner = inner.astype(jnp.float32)
+        parts = [table, nothing, inner] if layer == 2 else [table, inner, nothing]
+        packed = jnp.concatenate(parts, axis=1).astype(jnp.bfloat16)
         if layer == 0:
             first_ref[rows : rows + IB, :] = packed
         elif layer == 1:
@@ -43,18 +47,44 @@
             third_ref[...] = packed
 
 
-def dense_transposed(gathered_ref, table_row, outs, positions, run_blocks):
+def join_kernel(first_ref, second_ref, third_ref, message_ref):
+    rows = first_ref.shape[0] - IB
+    half = rows * KB
+    for p in range(message_ref.shape[0]):
+        message_ref[p, 0:rows, :] = first_ref[0:rows, :]
+        message_ref[p, rows : rows + IB, 0:half] = first_ref[rows : rows + IB, 0:half]
+        message_ref[p, rows : rows + IB, half:] = second_ref[:, 0:half]
+        message_ref[p, rows + IB :, 0:half] = third_ref[:, 0:half]
+        message_ref[p, rows + IB :, half : half + LANES] = (
+            first_ref[rows : rows + IB, half : half + LANES] + second_ref[:, half : half + LANES]
+        )
+        message_ref[p, rows + IB :, half + LANES :] = third_ref[:, half + LANES :]
+
+
+def dense_transposed(gathered_ref, layer, outs, positions, run_blocks):
     half = KB * outs
-    tables = [gathered_ref[p, table_row : table_row + IB, :].astype(jnp.float32) for p in range(positions)]
+    table_row, table_lane, index_lane, index_row = (
+        (outs, 0, half, 0),
+        (outs, half, half, KB),
+        (outs + IB, 0, half + LANES, 0),
+    )[layer]
+    tables = [
+        gathered_ref[p, table_row : table_row + IB, table_lane : table_lane + half].astype(jnp.float32)
+        for p in range(positions)
+    ]
+    inner = [
+        gathered_ref[p, outs + IB : outs + 2 * IB, index_lane : index_lane + LANES].astype(jnp.float32)
+        for p in range(positions)
+    ]
     rows = []
     for source in range(positions):
         w_parts, i_parts = [], []
         for target in range(positions):
             k = (source - target) % positions
             w_parts.append(tables[target][:, k * outs : (k + 1) * outs])
-            i_parts.append(tables[target][:, half + k * outs : half + (k + 1) * outs])
+            i_parts.append(inner[target][index_row + k : index_row + k + 1, 0:outs])
         w_row = jnp.concatenate(w_parts, axis=1)
-        i_row = jnp.concatenate(i_parts, axis=1)
+        i_row = jnp.broadcast_to(jnp.concatenate(i_parts, axis=1), w_row.shape)
         for b in range(run_blocks):
             rows.append(jnp.where(i_row == float(b), w_row, 0.0))
     return jnp.concatenate(rows, axis=0).astype(jnp.bfloat16)
@@ -74,7 +104,7 @@
     place = lax.axis_index("neu") // (lax.axis_size("neu") // KB)
     activity = jnp.concatenate([gathered_ref[p, 0:rows, :] for p in range(positions)], axis=0)
     for layer in range(3):
-        dense_t = dense_transposed(gathered_ref, rows + layer * IB, rows, positions, run_blocks)
+        dense_t = dense_transposed(gathered_ref, layer, rows, positions, run_blocks)
         activity = advance(dense_t, activity)
     last_ref[...] = activity.reshape(positions, rows, columns)
     activations_ref[...] = last_ref[place]
@@ -119,10 +149,16 @@
     )(image_values, image_mask, weights.transpose(0, 2, 3, 1), block_index)
     first = from_ahead(first, "neu", 3)
     second = from_ahead(second, "neu", 2)
-    message = jnp.concatenate([first, second, third], axis=0)
+    message = pl.pallas_call(
+        join_kernel,
+        in_specs=[vmem] * 3,
+        out_specs=vmem,
+        out_shape=pltpu.VMEM((KB, rows + 2 * IB, columns), jnp.bfloat16),
+        name="join",
+    )(*[pltpu.with_memory_space_constraint(piece, pltpu.VMEM) for piece in (first, second, third)])
     along_x = [[p * stride + g for p in range(KB)] for g in range(stride)]
     gathered = lax.all_to_all(
-        jnp.broadcast_to(message[None], (KB, *message.shape)), "neu", 0, 0, axis_index_groups=along_x, tiled=True
+        message, "neu", 0, 0, axis_index_groups=along_x, tiled=True
     )
     share = columns // KB
     activations, sums = pl.pallas_call(

time: 39.8 us -> 39.6 us (level)
  no operation moved by 1% of the time
where the time goes in v4:
time: 39.6 us; the launch traced here: 39.4 us
  blocking collectives  23.2 us (59%)
  starting transfers between devices  11.7 us (30%)
  Pallas kernels  2.44 us (6%)
  waiting for transfers between devices  1.42 us (4%)
  between operations  0.66 us (2%)
    all_to_all x1, blocking collectives, on_device(): lax.all_to_all(sums, 'neu', 0, 0, axis_index_groups=across, tiled=True)  15 us
    ppermute x2, starting transfers between devices, from_ahead(): return lax.ppermute(block, axis, route)  11.7 us
    all_to_all x1, blocking collectives, on_device(): lax.all_to_all(message, 'neu', 0, 0, axis_index_groups=along_x, tiled=True)  8.25 us
    ppermute x2, waiting for transfers between devices, from_ahead(): return lax.ppermute(block, axis, route)  1.42 us
    pallas_call x1, Pallas kernels, on_device(): pl.pallas_call(pack_kernel, in_specs=[vmem, vmem, vmem, smem], out_specs=...  1 us
  transfers between devices with their start and end apart: 2, of which 1 were waited for; matrix products, arithmetic and copies ran while one was open for 0% of the time, Pallas kernels for 0%

profile of v4, /device:TPU:1, one launch (start us, length us, event | category | flops | bytes accessed | tf_op | source)
XLA Modules:
  0.0 39.4 jit_solution(10332583759704631527)
XLA Ops:
  0.6 1.0 %pack.1 = (bf16[72,512]{1,0:T(8,128)(2,1)S(1)}, bf16[8,512]{1,0:T(8,128)(2,1)S(1)}, bf16[8,512]{1,0:T(8,128)(2,1)S(1)}) custom-call(bf16[64,512]{1,0:T(8,128)(2,1)} %values_ref.1, s32[64,512]{1,0:T(8,128)} %mask_ref.1, bf16[3,4,8,64]{3,2,1,0:T(8,128)(2,1)} %bitcast.2, s32[3,2,4]{2,1,0:T(2,128)} %index_ref.1), custom_call_target="tpu_custom_call" | custom-call | tf_op jit(solution)/shard_map/pack/pallas_call | solution.py:139
  1.6 8.7 %collective-permute-start = (bf16[72,512]{1,0:T(8,128)(2,1)S(1)}, bf16[72,512]{1,0:T(8,128)(2,1)S(1)}, u32[]{:S(2)}, u32[]{:S(2)}) collective-permute-start(bf16[72,512]{1,0:T(8,128)(2,1)S(1)} %get-tuple-element.9), channel_id=1, source_target_pairs={{3,0},{4,1},{5,2},{6,3},{7,4},{8,5},{9,6},{10,7},{11,8},{12,9},{13... | collective-permute-start | bytes 221192 | tf_op jit(solution)/shard_map/ppermute | solution.py:20
  10.3 3.0 %collective-permute-start.1 = (bf16[8,512]{1,0:T(8,128)(2,1)S(1)}, bf16[8,512]{1,0:T(8,128)(2,1)S(1)}, u32[]{:S(2)}, u32[]{:S(2)}) collective-permute-start(bf16[8,512]{1,0:T(8,128)(2,1)S(1)} %get-tuple-element.10), channel_id=1, source_target_pairs={{2,0},{3,1},{4,2},{5,3},{6,4},{7,5},{8,6},{9,7},{10,8},{11,9},{12,... | collective-permute-start | bytes 24584 | tf_op jit(solution)/shard_map/ppermute | solution.py:20
  13.3 1.4 %collective-permute-done.1.second_ref = bf16[8,512]{1,0:T(8,128)(2,1)S(1)} collective-permute-done((bf16[8,512]{1,0:T(8,128)(2,1)S(1)}, bf16[8,512]{1,0:T(8,128)(2,1)S(1)}, u32[]{:S(2)}, u32[]{:S(2)}) %collective-permute-start.1) | collective-permute-done | bytes 8224 | tf_op jit(solution)/shard_map/ppermute | solution.py:20
  14.7 0.0 collective-permute-done.first_ref
  14.7 8.3 %all_to_all.10.gathered_ref = bf16[4,80,512]{2,1,0:T(8,128)(2,1)S(1)} all-to-all(bf16[4,80,512]{2,1,0:T(8,128)(2,1)S(1)} %join.1), channel_id=1, replica_groups={{0,16,32,48},{1,17,33,49},{2,18,34,50},{3,19,35,51},{4,20,36,52},{5,21,..., dimensions={0} | all-to-all | bytes 655360 | tf_op jit(solution)/shard_map/all_to_all | solution.py:160
  23.0 0.8 %layers.1 = (bf16[64,512]{1,0:T(8,128)(2,1)S(1)}, f32[16,1,128]{2,1,0:T(1,128)S(1)}) custom-call(bf16[4,80,512]{2,1,0:T(8,128)(2,1)S(1)} %all_to_all.10.gathered_ref), custom_call_target="tpu_custom_call" | custom-call | tf_op jit(solution)/shard_map/layers/pallas_call | solution.py:164
  23.8 15.0 %all_to_all.11.parts_ref = f32[16,1,128]{2,1,0:T(1,128)S(1)} all-to-all(f32[16,1,128]{2,1,0:T(1,128)S(1)} %get-tuple-element.12), channel_id=1, replica_groups={{0,1,2,3,4,5,6,7,8,9,10,11,12,13,14,15},{16,17,18,19,20,21,22,23,24,25,..., dimensions={0} | all-to-all | bytes 16384 | tf_op jit(solution)/shard_map/all_to_all | solution.py:179
  38.7 0.7 %finish.1 = (bf16[64,512]{1,0:T(8,128)(2,1)}, f32[1,8]{1,0:T(1,128)}) custom-call(f32[16,1,128]{2,1,0:T(1,128)S(1)} %all_to_all.11.parts_ref, bf16[64,512]{1,0:T(8,128)(2,1)S(1)} %get-tuple-element.13.run_ref), custom_call_target="tpu_custom_call" | custom-call | tf_op jit(solution)/shard_map/finish/pallas_call | solution.py:180
  (1 shorter events, 0.0 us)
Async XLA Ops:
  1.6 13.1 %collective-permute-start = (bf16[72,512]{1,0:T(8,128)(2,1)S(1)}, bf16[72,512]{1,0:T(8,128)(2,1)S(1)}, u32[]{:S(2)}, u32[]{:S(2)}) collective-permute-start(bf16[72,512]{1,0:T(8,128)(2,1)S(1)} %get-tuple-element.9), channel_id=1, source_target_pairs={{3,0},{4,1},{5,2},{6,3},{7,4},{8,5},{9,6},{10,7},{11,8},{12,9},{13... | collective-permute-start | bytes 221192 | tf_op jit(solution)/shard_map/ppermute | solution.py:20
  10.3 4.4 %collective-permute-start.1 = (bf16[8,512]{1,0:T(8,128)(2,1)S(1)}, bf16[8,512]{1,0:T(8,128)(2,1)S(1)}, u32[]{:S(2)}, u32[]{:S(2)}) collective-permute-start(bf16[8,512]{1,0:T(8,128)(2,1)S(1)} %get-tuple-element.10), channel_id=1, source_target_pairs={{2,0},{3,1},{4,2},{5,3},{6,4},{7,5},{8,6},{9,7},{10,8},{11,9},{12,... | collective-permute-start | bytes 24584 | tf_op jit(solution)/shard_map/ppermute | solution.py:20

commit v5 on v4

--- a/solution.py
+++ b/solution.py
@@ -14,9 +14,10 @@
 ceiling = 32.0
 
 
-def from_ahead(block, axis, distance):
+def from_group_ahead(block, axis, distance):
     devices = lax.axis_size(axis)
-    route = [((i + distance) % devices, i) for i in range(devices)]
+    groups = devices // KB
+    route = [(i - i % groups + (i % groups + distance) % groups, i) for i in range(devices)]
     return lax.ppermute(block, axis, route)
 
 
@@ -101,10 +102,16 @@
     positions, _, columns = gathered_ref.shape
     rows = activations_ref.shape[0]
     run_blocks = rows // IB
-    place = lax.axis_index("neu") // (lax.axis_size("neu") // KB)
+    groups = lax.axis_size("neu") // KB
+    place = lax.axis_index("neu") // groups
+    group = lax.axis_index("neu") % groups
+    wraps = (None, group == groups - 3, group >= groups - 2)
     activity = jnp.concatenate([gathered_ref[p, 0:rows, :] for p in range(positions)], axis=0)
     for layer in range(3):
         dense_t = dense_transposed(gathered_ref, layer, rows, positions, run_blocks)
+        if layer > 0:
+            further = jnp.concatenate([activity[rows:], activity[:rows]], axis=0)
+            activity = jnp.where(wraps[layer], further, activity)
         activity = advance(dense_t, activity)
     last_ref[...] = activity.reshape(positions, rows, columns)
     activations_ref[...] = last_ref[place]
@@ -147,8 +154,8 @@
         ],
         name="pack",
     )(image_values, image_mask, weights.transpose(0, 2, 3, 1), block_index)
-    first = from_ahead(first, "neu", 3)
-    second = from_ahead(second, "neu", 2)
+    first = from_group_ahead(first, "neu", 3)
+    second = from_group_ahead(second, "neu", 2)
     message = pl.pallas_call(
         join_kernel,
         in_specs=[vmem] * 3,

time: 39.6 us -> 38 us (0.960)
  starting transfers between devices: 11.7 us -> 9.46 us
  waiting for transfers between devices: 1.42 us -> 3.61 us
  blocking collectives: 23.2 us -> 21.6 us
    ppermute x2, starting transfers between devices: 11.7 us -> 9.46 us  [from_group_ahead(): return lax.ppermute(block, axis, route)]
    ppermute x2, waiting for transfers between devices: 1.42 us -> 3.61 us  [from_group_ahead(): return lax.ppermute(block, axis, route)]
    all_to_all x1, blocking collectives: 15 us -> 13.3 us  [on_device(): lax.all_to_all(sums, 'neu', 0, 0, axis_index_groups=across, tiled=True)]
where the time goes in v5:
time: 38 us; the launch traced here: 37.8 us
  blocking collectives  21.6 us (57%)
  starting transfers between devices  9.46 us (25%)
  waiting for transfers between devices  3.61 us (10%)
  Pallas kernels  2.46 us (6%)
  between operations  0.66 us (2%)
    all_to_all x1, blocking collectives, on_device(): lax.all_to_all(sums, 'neu', 0, 0, axis_index_groups=across, tiled=True)  13.3 us
    ppermute x2, starting transfers between devices, from_group_ahead(): return lax.ppermute(block, axis, route)  9.46 us
    all_to_all x1, blocking collectives, on_device(): lax.all_to_all(message, 'neu', 0, 0, axis_index_groups=along_x, tiled=True)  8.27 us
    ppermute x2, waiting for transfers between devices, from_group_ahead(): return lax.ppermute(block, axis, route)  3.61 us
    pallas_call x1, Pallas kernels, on_device(): pl.pallas_call(pack_kernel, in_specs=[vmem, vmem, vmem, smem], out_specs=...  1 us
    pallas_call x1, Pallas kernels, on_device(): pl.pallas_call(layers_kernel, in_specs=[vmem], out_specs=[vmem, vmem], ou...  0.78 us
  transfers between devices with their start and end apart: 2, of which 1 were waited for; matrix products, arithmetic and copies ran while one was open for 0% of the time, Pallas kernels for 0%

profile of v5, /device:TPU:1, one launch (start us, length us, event | category | flops | bytes accessed | tf_op | source)
XLA Modules:
  0.0 37.8 jit_solution(14781007019093145985)
XLA Ops:
  0.6 1.0 %pack.1 = (bf16[72,512]{1,0:T(8,128)(2,1)S(1)}, bf16[8,512]{1,0:T(8,128)(2,1)S(1)}, bf16[8,512]{1,0:T(8,128)(2,1)S(1)}) custom-call(bf16[64,512]{1,0:T(8,128)(2,1)} %values_ref.1, s32[64,512]{1,0:T(8,128)} %mask_ref.1, bf16[3,4,8,64]{3,2,1,0:T(8,128)(2,1)} %bitcast.2, s32[3,2,4]{2,1,0:T(2,128)} %index_ref.1), custom_call_target="tpu_custom_call" | custom-call | tf_op jit(solution)/shard_map/pack/pallas_call | solution.py:146
  1.6 6.5 %collective-permute-start = (bf16[72,512]{1,0:T(8,128)(2,1)S(1)}, bf16[72,512]{1,0:T(8,128)(2,1)S(1)}, u32[]{:S(2)}, u32[]{:S(2)}) collective-permute-start(bf16[72,512]{1,0:T(8,128)(2,1)S(1)} %get-tuple-element.9), channel_id=1, source_target_pairs={{3,0},{4,1},{5,2},{6,3},{7,4},{8,5},{9,6},{10,7},{11,8},{12,9},{13... | collective-permute-start | bytes 221192 | tf_op jit(solution)/shard_map/ppermute | solution.py:21
  8.1 3.0 %collective-permute-start.1 = (bf16[8,512]{1,0:T(8,128)(2,1)S(1)}, bf16[8,512]{1,0:T(8,128)(2,1)S(1)}, u32[]{:S(2)}, u32[]{:S(2)}) collective-permute-start(bf16[8,512]{1,0:T(8,128)(2,1)S(1)} %get-tuple-element.10), channel_id=1, source_target_pairs={{2,0},{3,1},{4,2},{5,3},{6,4},{7,5},{8,6},{9,7},{10,8},{11,9},{12,... | collective-permute-start | bytes 24584 | tf_op jit(solution)/shard_map/ppermute | solution.py:21
  11.1 3.6 %collective-permute-done.1.second_ref = bf16[8,512]{1,0:T(8,128)(2,1)S(1)} collective-permute-done((bf16[8,512]{1,0:T(8,128)(2,1)S(1)}, bf16[8,512]{1,0:T(8,128)(2,1)S(1)}, u32[]{:S(2)}, u32[]{:S(2)}) %collective-permute-start.1) | collective-permute-done | bytes 8224 | tf_op jit(solution)/shard_map/ppermute | solution.py:21
  14.7 0.0 collective-permute-done.first_ref
  14.7 8.3 %all_to_all.10.gathered_ref = bf16[4,80,512]{2,1,0:T(8,128)(2,1)S(1)} all-to-all(bf16[4,80,512]{2,1,0:T(8,128)(2,1)S(1)} %join.1), channel_id=1, replica_groups={{0,16,32,48},{1,17,33,49},{2,18,34,50},{3,19,35,51},{4,20,36,52},{5,21,..., dimensions={0} | all-to-all | bytes 655360 | tf_op jit(solution)/shard_map/all_to_all | solution.py:167
  23.0 0.8 %layers.1 = (bf16[64,512]{1,0:T(8,128)(2,1)S(1)}, f32[16,1,128]{2,1,0:T(1,128)S(1)}) custom-call(bf16[4,80,512]{2,1,0:T(8,128)(2,1)S(1)} %all_to_all.10.gathered_ref), custom_call_target="tpu_custom_call" | custom-call | tf_op jit(solution)/shard_map/layers/pallas_call | solution.py:171
  23.8 13.3 %all_to_all.11.parts_ref = f32[16,1,128]{2,1,0:T(1,128)S(1)} all-to-all(f32[16,1,128]{2,1,0:T(1,128)S(1)} %get-tuple-element.12), channel_id=1, replica_groups={{0,1,2,3,4,5,6,7,8,9,10,11,12,13,14,15},{16,17,18,19,20,21,22,23,24,25,..., dimensions={0} | all-to-all | bytes 16384 | tf_op jit(solution)/shard_map/all_to_all | solution.py:186
  37.1 0.7 %finish.1 = (bf16[64,512]{1,0:T(8,128)(2,1)}, f32[1,8]{1,0:T(1,128)}) custom-call(f32[16,1,128]{2,1,0:T(1,128)S(1)} %all_to_all.11.parts_ref, bf16[64,512]{1,0:T(8,128)(2,1)S(1)} %get-tuple-element.13.run_ref), custom_call_target="tpu_custom_call" | custom-call | tf_op jit(solution)/shard_map/finish/pallas_call | solution.py:187
  (1 shorter events, 0.0 us)
Async XLA Ops:
  1.6 13.1 %collective-permute-start = (bf16[72,512]{1,0:T(8,128)(2,1)S(1)}, bf16[72,512]{1,0:T(8,128)(2,1)S(1)}, u32[]{:S(2)}, u32[]{:S(2)}) collective-permute-start(bf16[72,512]{1,0:T(8,128)(2,1)S(1)} %get-tuple-element.9), channel_id=1, source_target_pairs={{3,0},{4,1},{5,2},{6,3},{7,4},{8,5},{9,6},{10,7},{11,8},{12,9},{13... | collective-permute-start | bytes 221192 | tf_op jit(solution)/shard_map/ppermute | solution.py:21
  8.1 6.6 %collective-permute-start.1 = (bf16[8,512]{1,0:T(8,128)(2,1)S(1)}, bf16[8,512]{1,0:T(8,128)(2,1)S(1)}, u32[]{:S(2)}, u32[]{:S(2)}) collective-permute-start(bf16[8,512]{1,0:T(8,128)(2,1)S(1)} %get-tuple-element.10), channel_id=1, source_target_pairs={{2,0},{3,1},{4,2},{5,3},{6,4},{7,5},{8,6},{9,7},{10,8},{11,9},{12,... | collective-permute-start | bytes 24584 | tf_op jit(solution)/shard_map/ppermute | solution.py:21

commit v6 on v5

--- a/solution.py
+++ b/solution.py
@@ -129,7 +129,7 @@
     own = totals_ref.shape[-1]
     begin = (lax.axis_index("neu") % parts_ref.shape[0]) * own
     totals = jnp.broadcast_to(jnp.sum(parts_ref[...], axis=0), (8, share))
-    own_ref[...] = pltpu.roll(totals, share - begin, 1)[0:1, 0:own]
+    own_ref[...] = pltpu.roll(totals, (share - begin) % share, 1)[0:1, 0:own]
     own_out = pltpu.make_async_copy(own_ref, totals_ref, summed)
     own_out.start()
     out.wait()

time: 38 us -> 38 us (level)
  no operation moved by 1% of the time
where the time goes in v6:
time: 38 us; the launch traced here: 37.8 us
  blocking collectives  21.6 us (57%)
  starting transfers between devices  9.46 us (25%)
  waiting for transfers between devices  3.61 us (10%)
  Pallas kernels  2.46 us (6%)
  between operations  0.66 us (2%)
    all_to_all x1, blocking collectives, on_device(): lax.all_to_all(sums, 'neu', 0, 0, axis_index_groups=across, tiled=True)  13.3 us
    ppermute x2, starting transfers between devices, from_group_ahead(): return lax.ppermute(block, axis, route)  9.46 us
    all_to_all x1, blocking collectives, on_device(): lax.all_to_all(message, 'neu', 0, 0, axis_index_groups=along_x, tiled=True)  8.27 us
    ppermute x2, waiting for transfers between devices, from_group_ahead(): return lax.ppermute(block, axis, route)  3.61 us
    pallas_call x1, Pallas kernels, on_device(): pl.pallas_call(pack_kernel, in_specs=[vmem, vmem, vmem, smem], out_specs=...  1 us
    pallas_call x1, Pallas kernels, on_device(): pl.pallas_call(layers_kernel, in_specs=[vmem], out_specs=[vmem, vmem], ou...  0.78 us
  transfers between devices with their start and end apart: 2, of which 1 were waited for; matrix products, arithmetic and copies ran while one was open for 0% of the time, Pallas kernels for 0%

profile of v6, /device:TPU:1, one launch (start us, length us, event | category | flops | bytes accessed | tf_op | source)
XLA Modules:
  0.0 37.8 jit_solution(1683126845374448156)
XLA Ops:
  0.6 1.0 %pack.1 = (bf16[72,512]{1,0:T(8,128)(2,1)S(1)}, bf16[8,512]{1,0:T(8,128)(2,1)S(1)}, bf16[8,512]{1,0:T(8,128)(2,1)S(1)}) custom-call(bf16[64,512]{1,0:T(8,128)(2,1)} %values_ref.1, s32[64,512]{1,0:T(8,128)} %mask_ref.1, bf16[3,4,8,64]{3,2,1,0:T(8,128)(2,1)} %bitcast.2, s32[3,2,4]{2,1,0:T(2,128)} %index_ref.1), custom_call_target="tpu_custom_call" | custom-call | tf_op jit(solution)/shard_map/pack/pallas_call | solution.py:146
  1.6 6.5 %collective-permute-start = (bf16[72,512]{1,0:T(8,128)(2,1)S(1)}, bf16[72,512]{1,0:T(8,128)(2,1)S(1)}, u32[]{:S(2)}, u32[]{:S(2)}) collective-permute-start(bf16[72,512]{1,0:T(8,128)(2,1)S(1)} %get-tuple-element.9), channel_id=1, source_target_pairs={{3,0},{4,1},{5,2},{6,3},{7,4},{8,5},{9,6},{10,7},{11,8},{12,9},{13... | collective-permute-start | bytes 221192 | tf_op jit(solution)/shard_map/ppermute | solution.py:21
  8.1 3.0 %collective-permute-start.1 = (bf16[8,512]{1,0:T(8,128)(2,1)S(1)}, bf16[8,512]{1,0:T(8,128)(2,1)S(1)}, u32[]{:S(2)}, u32[]{:S(2)}) collective-permute-start(bf16[8,512]{1,0:T(8,128)(2,1)S(1)} %get-tuple-element.10), channel_id=1, source_target_pairs={{2,0},{3,1},{4,2},{5,3},{6,4},{7,5},{8,6},{9,7},{10,8},{11,9},{12,... | collective-permute-start | bytes 24584 | tf_op jit(solution)/shard_map/ppermute | solution.py:21
  11.1 3.6 %collective-permute-done.1.second_ref = bf16[8,512]{1,0:T(8,128)(2,1)S(1)} collective-permute-done((bf16[8,512]{1,0:T(8,128)(2,1)S(1)}, bf16[8,512]{1,0:T(8,128)(2,1)S(1)}, u32[]{:S(2)}, u32[]{:S(2)}) %collective-permute-start.1) | collective-permute-done | bytes 8224 | tf_op jit(solution)/shard_map/ppermute | solution.py:21
  14.7 0.0 collective-permute-done.first_ref
  14.7 8.3 %all_to_all.10.gathered_ref = bf16[4,80,512]{2,1,0:T(8,128)(2,1)S(1)} all-to-all(bf16[4,80,512]{2,1,0:T(8,128)(2,1)S(1)} %join.1), channel_id=1, replica_groups={{0,16,32,48},{1,17,33,49},{2,18,34,50},{3,19,35,51},{4,20,36,52},{5,21,..., dimensions={0} | all-to-all | bytes 655360 | tf_op jit(solution)/shard_map/all_to_all | solution.py:167
  23.0 0.8 %layers.1 = (bf16[64,512]{1,0:T(8,128)(2,1)S(1)}, f32[16,1,128]{2,1,0:T(1,128)S(1)}) custom-call(bf16[4,80,512]{2,1,0:T(8,128)(2,1)S(1)} %all_to_all.10.gathered_ref), custom_call_target="tpu_custom_call" | custom-call | tf_op jit(solution)/shard_map/layers/pallas_call | solution.py:171
  23.8 13.3 %all_to_all.11.parts_ref = f32[16,1,128]{2,1,0:T(1,128)S(1)} all-to-all(f32[16,1,128]{2,1,0:T(1,128)S(1)} %get-tuple-element.12), channel_id=1, replica_groups={{0,1,2,3,4,5,6,7,8,9,10,11,12,13,14,15},{16,17,18,19,20,21,22,23,24,25,..., dimensions={0} | all-to-all | bytes 16384 | tf_op jit(solution)/shard_map/all_to_all | solution.py:186
  37.1 0.7 %finish.1 = (bf16[64,512]{1,0:T(8,128)(2,1)}, f32[1,8]{1,0:T(1,128)}) custom-call(f32[16,1,128]{2,1,0:T(1,128)S(1)} %all_to_all.11.parts_ref, bf16[64,512]{1,0:T(8,128)(2,1)S(1)} %get-tuple-element.13.run_ref), custom_call_target="tpu_custom_call" | custom-call | tf_op jit(solution)/shard_map/finish/pallas_call | solution.py:187
  (1 shorter events, 0.0 us)
Async XLA Ops:
  1.6 13.1 %collective-permute-start = (bf16[72,512]{1,0:T(8,128)(2,1)S(1)}, bf16[72,512]{1,0:T(8,128)(2,1)S(1)}, u32[]{:S(2)}, u32[]{:S(2)}) collective-permute-start(bf16[72,512]{1,0:T(8,128)(2,1)S(1)} %get-tuple-element.9), channel_id=1, source_target_pairs={{3,0},{4,1},{5,2},{6,3},{7,4},{8,5},{9,6},{10,7},{11,8},{12,9},{13... | collective-permute-start | bytes 221192 | tf_op jit(solution)/shard_map/ppermute | solution.py:21
  8.1 6.6 %collective-permute-start.1 = (bf16[8,512]{1,0:T(8,128)(2,1)S(1)}, bf16[8,512]{1,0:T(8,128)(2,1)S(1)}, u32[]{:S(2)}, u32[]{:S(2)}) collective-permute-start(bf16[8,512]{1,0:T(8,128)(2,1)S(1)} %get-tuple-element.10), channel_id=1, source_target_pairs={{2,0},{3,1},{4,2},{5,3},{6,4},{7,5},{8,6},{9,7},{10,8},{11,9},{12,... | collective-permute-start | bytes 24584 | tf_op jit(solution)/shard_map/ppermute | solution.py:21

commit v7 on v6

--- a/solution.py
+++ b/solution.py
@@ -9,6 +9,7 @@
 IB = 8
 OB = 32
 LANES = 128
+FIRST_X = 2
 
 bias_value = 0.35
 ceiling = 32.0
@@ -114,7 +115,7 @@
             activity = jnp.where(wraps[layer], further, activity)
         activity = advance(dense_t, activity)
     last_ref[...] = activity.reshape(positions, rows, columns)
-    activations_ref[...] = last_ref[place]
+    activations_ref[...] = last_ref[(place + KB - FIRST_X) % KB]
     totals = jnp.sum(activity.astype(jnp.float32), axis=0, keepdims=True)
     share = columns // positions
     for p in range(positions):
@@ -163,7 +164,7 @@
         out_shape=pltpu.VMEM((KB, rows + 2 * IB, columns), jnp.bfloat16),
         name="join",
     )(*[pltpu.with_memory_space_constraint(piece, pltpu.VMEM) for piece in (first, second, third)])
-    along_x = [[p * stride + g for p in range(KB)] for g in range(stride)]
+    along_x = [[(p + FIRST_X) % KB * stride + g for p in range(KB)] for g in range(stride)]
     gathered = lax.all_to_all(
         message, "neu", 0, 0, axis_index_groups=along_x, tiled=True
     )
@@ -182,7 +183,8 @@
         ],
         name="layers",
     )(pltpu.with_memory_space_constraint(gathered, pltpu.VMEM))
-    across = [[p * stride + g for g in range(stride)] for p in range(KB)]
+    farthest = stride // 2 + 1
+    across = [[p * stride + (g + farthest) % stride for g in range(stride)] for p in range(KB)]
     parts = lax.all_to_all(sums, "neu", 0, 0, axis_index_groups=across, tiled=True)
     activations, totals = pl.pallas_call(
         finish_kernel,

time: 38 us -> 34.8 us (0.916)
  blocking collectives: 21.6 us -> 18.4 us
    all_to_all x1, blocking collectives: 13.3 us -> 10.8 us  [on_device(): lax.all_to_all(sums, 'neu', 0, 0, axis_index_groups=across, tiled=True)]
    all_to_all x1, blocking collectives: 8.27 us -> 7.53 us  [on_device(): lax.all_to_all(message, 'neu', 0, 0, axis_index_groups=along_x, tiled=True)]
where the time goes in v7:
time: 34.8 us; the launch traced here: 34.6 us
  blocking collectives  18.4 us (53%)
  starting transfers between devices  9.46 us (27%)
  waiting for transfers between devices  3.61 us (10%)
  Pallas kernels  2.46 us (7%)
  between operations  0.66 us (2%)
    all_to_all x1, blocking collectives, on_device(): lax.all_to_all(sums, 'neu', 0, 0, axis_index_groups=across, tiled=True)  10.8 us
    ppermute x2, starting transfers between devices, from_group_ahead(): return lax.ppermute(block, axis, route)  9.46 us
    all_to_all x1, blocking collectives, on_device(): lax.all_to_all(message, 'neu', 0, 0, axis_index_groups=along_x, tiled=True)  7.53 us
    ppermute x2, waiting for transfers between devices, from_group_ahead(): return lax.ppermute(block, axis, route)  3.61 us
    pallas_call x1, Pallas kernels, on_device(): pl.pallas_call(pack_kernel, in_specs=[vmem, vmem, vmem, smem], out_specs=...  1 us
    pallas_call x1, Pallas kernels, on_device(): pl.pallas_call(layers_kernel, in_specs=[vmem], out_specs=[vmem, vmem], ou...  0.78 us
  transfers between devices with their start and end apart: 2, of which 1 were waited for; matrix products, arithmetic and copies ran while one was open for 0% of the time, Pallas kernels for 0%

profile of v7, /device:TPU:1, one launch (start us, length us, event | category | flops | bytes accessed | tf_op | source)
XLA Modules:
  0.0 34.6 jit_solution(16374353090329029031)
XLA Ops:
  0.6 1.0 %pack.1 = (bf16[72,512]{1,0:T(8,128)(2,1)S(1)}, bf16[8,512]{1,0:T(8,128)(2,1)S(1)}, bf16[8,512]{1,0:T(8,128)(2,1)S(1)}) custom-call(bf16[64,512]{1,0:T(8,128)(2,1)} %values_ref.1, s32[64,512]{1,0:T(8,128)} %mask_ref.1, bf16[3,4,8,64]{3,2,1,0:T(8,128)(2,1)} %bitcast.2, s32[3,2,4]{2,1,0:T(2,128)} %index_ref.1), custom_call_target="tpu_custom_call" | custom-call | tf_op jit(solution)/shard_map/pack/pallas_call | solution.py:147
  1.6 6.5 %collective-permute-start = (bf16[72,512]{1,0:T(8,128)(2,1)S(1)}, bf16[72,512]{1,0:T(8,128)(2,1)S(1)}, u32[]{:S(2)}, u32[]{:S(2)}) collective-permute-start(bf16[72,512]{1,0:T(8,128)(2,1)S(1)} %get-tuple-element.9), channel_id=1, source_target_pairs={{3,0},{4,1},{5,2},{6,3},{7,4},{8,5},{9,6},{10,7},{11,8},{12,9},{13... | collective-permute-start | bytes 221192 | tf_op jit(solution)/shard_map/ppermute | solution.py:22
  8.1 3.0 %collective-permute-start.1 = (bf16[8,512]{1,0:T(8,128)(2,1)S(1)}, bf16[8,512]{1,0:T(8,128)(2,1)S(1)}, u32[]{:S(2)}, u32[]{:S(2)}) collective-permute-start(bf16[8,512]{1,0:T(8,128)(2,1)S(1)} %get-tuple-element.10), channel_id=1, source_target_pairs={{2,0},{3,1},{4,2},{5,3},{6,4},{7,5},{8,6},{9,7},{10,8},{11,9},{12,... | collective-permute-start | bytes 24584 | tf_op jit(solution)/shard_map/ppermute | solution.py:22
  11.1 3.6 %collective-permute-done.1.second_ref = bf16[8,512]{1,0:T(8,128)(2,1)S(1)} collective-permute-done((bf16[8,512]{1,0:T(8,128)(2,1)S(1)}, bf16[8,512]{1,0:T(8,128)(2,1)S(1)}, u32[]{:S(2)}, u32[]{:S(2)}) %collective-permute-start.1) | collective-permute-done | bytes 8224 | tf_op jit(solution)/shard_map/ppermute | solution.py:22
  14.7 0.0 collective-permute-done.first_ref
  14.7 7.5 %all_to_all.10.gathered_ref = bf16[4,80,512]{2,1,0:T(8,128)(2,1)S(1)} all-to-all(bf16[4,80,512]{2,1,0:T(8,128)(2,1)S(1)} %join.1), channel_id=1, replica_groups={{32,48,0,16},{33,49,1,17},{34,50,2,18},{35,51,3,19},{36,52,4,20},{37,53..., dimensions={0} | all-to-all | bytes 655360 | tf_op jit(solution)/shard_map/all_to_all | solution.py:168
  22.3 0.8 %layers.1 = (bf16[64,512]{1,0:T(8,128)(2,1)S(1)}, f32[16,1,128]{2,1,0:T(1,128)S(1)}) custom-call(bf16[4,80,512]{2,1,0:T(8,128)(2,1)S(1)} %all_to_all.10.gathered_ref), custom_call_target="tpu_custom_call" | custom-call | tf_op jit(solution)/shard_map/layers/pallas_call | solution.py:172
  23.1 10.8 %all_to_all.11.parts_ref = f32[16,1,128]{2,1,0:T(1,128)S(1)} all-to-all(f32[16,1,128]{2,1,0:T(1,128)S(1)} %get-tuple-element.12), channel_id=1, replica_groups={{9,10,11,12,13,14,15,0,1,2,3,4,5,6,7,8},{25,26,27,28,29,30,31,16,17,18,..., dimensions={0} | all-to-all | bytes 16384 | tf_op jit(solution)/shard_map/all_to_all | solution.py:188
  33.9 0.7 %finish.1 = (bf16[64,512]{1,0:T(8,128)(2,1)}, f32[1,8]{1,0:T(1,128)}) custom-call(f32[16,1,128]{2,1,0:T(1,128)S(1)} %all_to_all.11.parts_ref, bf16[64,512]{1,0:T(8,128)(2,1)S(1)} %get-tuple-element.13.run_ref), custom_call_target="tpu_custom_call" | custom-call | tf_op jit(solution)/shard_map/finish/pallas_call | solution.py:189
  (1 shorter events, 0.0 us)
Async XLA Ops:
  1.6 13.1 %collective-permute-start = (bf16[72,512]{1,0:T(8,128)(2,1)S(1)}, bf16[72,512]{1,0:T(8,128)(2,1)S(1)}, u32[]{:S(2)}, u32[]{:S(2)}) collective-permute-start(bf16[72,512]{1,0:T(8,128)(2,1)S(1)} %get-tuple-element.9), channel_id=1, source_target_pairs={{3,0},{4,1},{5,2},{6,3},{7,4},{8,5},{9,6},{10,7},{11,8},{12,9},{13... | collective-permute-start | bytes 221192 | tf_op jit(solution)/shard_map/ppermute | solution.py:22
  8.1 6.6 %collective-permute-start.1 = (bf16[8,512]{1,0:T(8,128)(2,1)S(1)}, bf16[8,512]{1,0:T(8,128)(2,1)S(1)}, u32[]{:S(2)}, u32[]{:S(2)}) collective-permute-start(bf16[8,512]{1,0:T(8,128)(2,1)S(1)} %get-tuple-element.10), channel_id=1, source_target_pairs={{2,0},{3,1},{4,2},{5,3},{6,4},{7,5},{8,6},{9,7},{10,8},{11,9},{12,... | collective-permute-start | bytes 24584 | tf_op jit(solution)/shard_map/ppermute | solution.py:22

commit v8 on v7

--- a/solution.py
+++ b/solution.py
@@ -9,7 +9,7 @@
 IB = 8
 OB = 32
 LANES = 128
-FIRST_X = 2
+ALONG_X = (2, 1, 3, 0)
 
 bias_value = 0.35
 ceiling = 32.0
@@ -82,7 +82,7 @@
     for source in range(positions):
         w_parts, i_parts = [], []
         for target in range(positions):
-            k = (source - target) % positions
+            k = (ALONG_X[source] - ALONG_X[target]) % positions
             w_parts.append(tables[target][:, k * outs : (k + 1) * outs])
             i_parts.append(inner[target][index_row + k : index_row + k + 1, 0:outs])
         w_row = jnp.concatenate(w_parts, axis=1)
@@ -111,11 +111,15 @@
     for layer in range(3):
         dense_t = dense_transposed(gathered_ref, layer, rows, positions, run_blocks)
         if layer > 0:
-            further = jnp.concatenate([activity[rows:], activity[:rows]], axis=0)
+            nexts = [ALONG_X.index((x + 1) % positions) for x in ALONG_X]
+            further = jnp.concatenate([activity[p * rows : (p + 1) * rows] for p in nexts], axis=0)
             activity = jnp.where(wraps[layer], further, activity)
         activity = advance(dense_t, activity)
     last_ref[...] = activity.reshape(positions, rows, columns)
-    activations_ref[...] = last_ref[(place + KB - FIRST_X) % KB]
+    position = 0
+    for p in range(1, positions):
+        position = jnp.where(place == ALONG_X[p], p, position)
+    activations_ref[...] = last_ref[position]
     totals = jnp.sum(activity.astype(jnp.float32), axis=0, keepdims=True)
     share = columns // positions
     for p in range(positions):
@@ -164,7 +168,7 @@
         out_shape=pltpu.VMEM((KB, rows + 2 * IB, columns), jnp.bfloat16),
         name="join",
     )(*[pltpu.with_memory_space_constraint(piece, pltpu.VMEM) for piece in (first, second, third)])
-    along_x = [[(p + FIRST_X) % KB * stride + g for p in range(KB)] for g in range(stride)]
+    along_x = [[x * stride + g for x in ALONG_X] for g in range(stride)]
     gathered = lax.all_to_all(
         message, "neu", 0, 0, axis_index_groups=along_x, tiled=True
     )

time: 34.8 us -> 34.4 us (0.989)
  blocking collectives: 18.4 us -> 18 us
where the time goes in v8:
time: 34.4 us; the launch traced here: 34.2 us
  blocking collectives  18 us (52%)
  starting transfers between devices  9.46 us (28%)
  waiting for transfers between devices  3.61 us (10%)
  Pallas kernels  2.48 us (7%)
  between operations  0.66 us (2%)
    all_to_all x1, blocking collectives, on_device(): lax.all_to_all(sums, 'neu', 0, 0, axis_index_groups=across, tiled=True)  10.7 us
    ppermute x2, starting transfers between devices, from_group_ahead(): return lax.ppermute(block, axis, route)  9.46 us
    all_to_all x1, blocking collectives, on_device(): lax.all_to_all(message, 'neu', 0, 0, axis_index_groups=along_x, tiled=True)  7.25 us
    ppermute x2, waiting for transfers between devices, from_group_ahead(): return lax.ppermute(block, axis, route)  3.61 us
    pallas_call x1, Pallas kernels, on_device(): pl.pallas_call(pack_kernel, in_specs=[vmem, vmem, vmem, smem], out_specs=...  1 us
    pallas_call x1, Pallas kernels, on_device(): pl.pallas_call(layers_kernel, in_specs=[vmem], out_specs=[vmem, vmem], ou...  0.8 us
  transfers between devices with their start and end apart: 2, of which 1 were waited for; matrix products, arithmetic and copies ran while one was open for 0% of the time, Pallas kernels for 0%

profile of v8, /device:TPU:1, one launch (start us, length us, event | category | flops | bytes accessed | tf_op | source)
XLA Modules:
  0.0 34.2 jit_solution(16588261235914928395)
XLA Ops:
  0.6 1.0 %pack.1 = (bf16[72,512]{1,0:T(8,128)(2,1)S(1)}, bf16[8,512]{1,0:T(8,128)(2,1)S(1)}, bf16[8,512]{1,0:T(8,128)(2,1)S(1)}) custom-call(bf16[64,512]{1,0:T(8,128)(2,1)} %values_ref.1, s32[64,512]{1,0:T(8,128)} %mask_ref.1, bf16[3,4,8,64]{3,2,1,0:T(8,128)(2,1)} %bitcast.2, s32[3,2,4]{2,1,0:T(2,128)} %index_ref.1), custom_call_target="tpu_custom_call" | custom-call | tf_op jit(solution)/shard_map/pack/pallas_call | solution.py:151
  1.6 6.5 %collective-permute-start = (bf16[72,512]{1,0:T(8,128)(2,1)S(1)}, bf16[72,512]{1,0:T(8,128)(2,1)S(1)}, u32[]{:S(2)}, u32[]{:S(2)}) collective-permute-start(bf16[72,512]{1,0:T(8,128)(2,1)S(1)} %get-tuple-element.9), channel_id=1, source_target_pairs={{3,0},{4,1},{5,2},{6,3},{7,4},{8,5},{9,6},{10,7},{11,8},{12,9},{13... | collective-permute-start | bytes 221192 | tf_op jit(solution)/shard_map/ppermute | solution.py:22
  8.1 3.0 %collective-permute-start.1 = (bf16[8,512]{1,0:T(8,128)(2,1)S(1)}, bf16[8,512]{1,0:T(8,128)(2,1)S(1)}, u32[]{:S(2)}, u32[]{:S(2)}) collective-permute-start(bf16[8,512]{1,0:T(8,128)(2,1)S(1)} %get-tuple-element.10), channel_id=1, source_target_pairs={{2,0},{3,1},{4,2},{5,3},{6,4},{7,5},{8,6},{9,7},{10,8},{11,9},{12,... | collective-permute-start | bytes 24584 | tf_op jit(solution)/shard_map/ppermute | solution.py:22
  11.1 3.6 %collective-permute-done.1.second_ref = bf16[8,512]{1,0:T(8,128)(2,1)S(1)} collective-permute-done((bf16[8,512]{1,0:T(8,128)(2,1)S(1)}, bf16[8,512]{1,0:T(8,128)(2,1)S(1)}, u32[]{:S(2)}, u32[]{:S(2)}) %collective-permute-start.1) | collective-permute-done | bytes 8224 | tf_op jit(solution)/shard_map/ppermute | solution.py:22
  14.7 0.0 collective-permute-done.first_ref
  14.7 7.2 %all_to_all.10.gathered_ref = bf16[4,80,512]{2,1,0:T(8,128)(2,1)S(1)} all-to-all(bf16[4,80,512]{2,1,0:T(8,128)(2,1)S(1)} %join.1), channel_id=1, replica_groups={{32,16,48,0},{33,17,49,1},{34,18,50,2},{35,19,51,3},{36,20,52,4},{37,21..., dimensions={0} | all-to-all | bytes 655360 | tf_op jit(solution)/shard_map/all_to_all | solution.py:172
  22.0 0.8 %layers.1 = (bf16[64,512]{1,0:T(8,128)(2,1)S(1)}, f32[16,1,128]{2,1,0:T(1,128)S(1)}) custom-call(bf16[4,80,512]{2,1,0:T(8,128)(2,1)S(1)} %all_to_all.10.gathered_ref), custom_call_target="tpu_custom_call" | custom-call | tf_op jit(solution)/shard_map/layers/pallas_call | solution.py:176
  22.8 10.7 %all_to_all.11.parts_ref = f32[16,1,128]{2,1,0:T(1,128)S(1)} all-to-all(f32[16,1,128]{2,1,0:T(1,128)S(1)} %get-tuple-element.12), channel_id=1, replica_groups={{9,10,11,12,13,14,15,0,1,2,3,4,5,6,7,8},{25,26,27,28,29,30,31,16,17,18,..., dimensions={0} | all-to-all | bytes 16384 | tf_op jit(solution)/shard_map/all_to_all | solution.py:192
  33.5 0.7 %finish.1 = (bf16[64,512]{1,0:T(8,128)(2,1)}, f32[1,8]{1,0:T(1,128)}) custom-call(f32[16,1,128]{2,1,0:T(1,128)S(1)} %all_to_all.11.parts_ref, bf16[64,512]{1,0:T(8,128)(2,1)S(1)} %get-tuple-element.13.run_ref), custom_call_target="tpu_custom_call" | custom-call | tf_op jit(solution)/shard_map/finish/pallas_call | solution.py:193
  (1 shorter events, 0.0 us)
Async XLA Ops:
  1.6 13.1 %collective-permute-start = (bf16[72,512]{1,0:T(8,128)(2,1)S(1)}, bf16[72,512]{1,0:T(8,128)(2,1)S(1)}, u32[]{:S(2)}, u32[]{:S(2)}) collective-permute-start(bf16[72,512]{1,0:T(8,128)(2,1)S(1)} %get-tuple-element.9), channel_id=1, source_target_pairs={{3,0},{4,1},{5,2},{6,3},{7,4},{8,5},{9,6},{10,7},{11,8},{12,9},{13... | collective-permute-start | bytes 221192 | tf_op jit(solution)/shard_map/ppermute | solution.py:22
  8.1 6.6 %collective-permute-start.1 = (bf16[8,512]{1,0:T(8,128)(2,1)S(1)}, bf16[8,512]{1,0:T(8,128)(2,1)S(1)}, u32[]{:S(2)}, u32[]{:S(2)}) collective-permute-start(bf16[8,512]{1,0:T(8,128)(2,1)S(1)} %get-tuple-element.10), channel_id=1, source_target_pairs={{2,0},{3,1},{4,2},{5,3},{6,4},{7,5},{8,6},{9,7},{10,8},{11,9},{12,... | collective-permute-start | bytes 24584 | tf_op jit(solution)/shard_map/ppermute | solution.py:22
